TPU v7x, 256 devices: a whole 4x4x8 slice. The times are simulated.
256 devices in a mesh: grp: 16 (over z, core), blk: 16 (over x, y).
Axes of the slice: x: 4, y: 4, z: 8, core: 2. Of those that a mesh axis runs over, the one named last changes fastest.
Arguments:
- patches: float32 [2048, 32, 1024], P(('grp', 'blk')), may hold values from -6 to 6
- counts: int32 [256], P(('grp', 'blk')), may hold values from 1 to 8
- moves: int32 [256, 4], P(('grp', 'blk')), may hold values from 0 to 3, as said below
- tags: int32 [16, 128], P('grp'), may hold values from 0 to 3
Outputs:
- fine: bfloat16 [2048, 64, 4096], P(('grp', 'blk'))
Inputs may be any that keep to these rules, and one draw needn't show every extreme that they name: `moves`: each device holds between 1 and 8 live patches before and after every diffusion step, and hands on fewer patches than it holds at that step; in every draw some device hands on exactly 3 patches in some step.
All inputs are finite; a program needn't handle non-finite values.
Results may differ from a plain program's by a relative error of at most 0.001.
Values sent between devices are 32-bit elements; how exact they have to be, the bound alone decides.
A program may use at most 128 MiB of HBM per device.

v0:
```python
import jax
import jax.numpy as jnp
from jax import lax
from jax.sharding import PartitionSpec as P

MOST = 3
STEPS = 4


def passed_along(block, axis, distance):
    devices = range(lax.axis_size(axis))
    route = [((i - distance) % len(devices), i) for i in devices]
    return lax.ppermute(block, axis, route)


def from_everyone(x, axis):
    devices = lax.axis_size(axis)
    return lax.all_to_all(jnp.broadcast_to(x[None], (devices, *x.shape)), axis, 0, 0, tiled=True)


def combined_pairwise(pieces, combine):
    while len(jax.tree.leaves(pieces)[0]) > 1:
        pieces = jax.vmap(combine)(*(pieces[side::2] for side in (0, 1)))
    return pieces[0]


def carried_in(x, axis, combine, identity):
    devices, place = (lax.axis_size(axis), lax.axis_index(axis))
    passed = jnp.arange(devices) < place

    def kept(part, zero, own):
        part = jnp.where(
            passed.reshape(-1, *(1 for _ in own.shape)), part, jnp.asarray(zero, own.dtype)
        )
        return part

    pieces = from_everyone(x, axis)
    return combined_pairwise(kept(pieces, identity, x), combine)


def from_behind(x, axis, by):
    devices = lax.axis_size(axis)
    pairs = [(i, i + by) for i in range(devices) if 0 <= i + by < devices]
    return lax.ppermute(x, axis, pairs)


def refine_table(edge, margin):
    finer = jnp.arange(2 * edge)[:, None]
    coarse = jnp.arange(edge + 2 * margin)[None, :]
    home = finer // 2 + margin
    side = home + 2 * (finer % 2) - 1
    return (0.75 * (coarse == home) + 0.25 * (coarse == side)).astype(jnp.float32)


def refine(extended, edge):
    number = extended.shape[0]
    cube = extended.reshape(number, edge + 2, edge, edge)
    across = refine_table(edge, 1)
    inner = refine_table(edge, 0)
    highest = lax.Precision.HIGHEST
    first = jnp.einsum("fx,pxyz->pfyz", across, cube, precision=highest)
    second = jnp.einsum("gy,pfyz->pfgz", inner, first, precision=highest)
    third = jnp.einsum("hz,pfgz->pfgh", inner, second, precision=highest)
    return third.reshape(number, 2 * edge, 4 * edge * edge)


def tag_factors(tag_row, offset, capacity):
    position = offset + jnp.arange(capacity)
    boxes = jnp.arange(tag_row.shape[0])
    picked = jnp.sum(jnp.where(position[:, None] == boxes[None, :], tag_row[None, :], 0), axis=1)
    return 1.0 + 0.5 * picked.astype(jnp.float32)


def finish(work, live, lower, upper, factors):
    capacity, edge = (work.shape[0], work.shape[1])
    slots = jnp.arange(capacity)
    below = jnp.concatenate([lower[None], work[:-1, edge - 1]], 0)
    above = jnp.concatenate([work[1:, 0], upper[None]], 0)
    above = jnp.where((slots == live - 1)[:, None], upper[None], above)
    extended = jnp.concatenate([below[:, None], work, above[:, None]], 1)
    refined = refine(extended, edge)
    scaled = refined * factors[:, None, None]
    return jnp.where((slots < live)[:, None, None], scaled, 0.0).astype(jnp.bfloat16)


def add_counts(earlier, later):
    return earlier + later


def body(patches, counts, moves, tags):
    capacity, edge = (patches.shape[0], patches.shape[1])
    live = counts[0]
    padding = jnp.zeros((MOST,) + patches.shape[1:], patches.dtype)
    field = jnp.concatenate([patches, padding], 0)
    earlier = passed_along(moves, "blk", 1)
    for step in range(STEPS):
        start = live - moves[0, step]
        parcel = lax.dynamic_slice_in_dim(field, start, MOST, 0)
        arrived = passed_along(parcel, "blk", 1)
        field = lax.dynamic_update_slice_in_dim(field, arrived, start, 0)
        live = start + earlier[0, step]
    work = field[:capacity]
    offset = carried_in(live.reshape(1), "blk", add_counts, jnp.zeros((1,), jnp.int32))[0]
    top_patch = lax.dynamic_index_in_dim(work, live - 1, 0, keepdims=False)
    lower = from_behind(top_patch[edge - 1], ("grp", "blk"), 1)
    upper = from_behind(work[0, 0], ("grp", "blk"), -1)
    return finish(work, live, lower, upper, tag_factors(tags[0], offset, capacity))


def solution(mesh):
    in_specs = (
        P(("grp", "blk"), None, None),
        P(("grp", "blk")),
        P(("grp", "blk"), None),
        P("grp", None),
    )
    out_specs = P(("grp", "blk"), None, None)
    return jax.shard_map(body, mesh=mesh, in_specs=in_specs, out_specs=out_specs, check_vma=False)
```

profile of v0, /device:TPU:127, one launch (start us, length us, event | category | flops | bytes accessed | tf_op | source)
XLA Modules:
  0.0 157.7 jit_solution(4098431264649642860)
XLA Ops:
  0.0 1.5 fusion.46
  2.7 0.0 copy-start
  2.7 1.0 pad_dynamic-slice_fusion
  3.7 0.1 collective-permute-start.1
  3.8 1.1 collective-permute-start
  5.0 1.4 concatenate.32
  6.3 7.5 %collective-permute-done = s32[1,4]{1,0:T(1,128)S(1)} collective-permute-done((s32[1,4]{1,0:T(1,128)}, s32[1,4]{1,0:T(1,128)S(1)}, u32[]{:S(2)}, u32[]{:S(2)}) %collective-permute-start) | collective-permute-done | bytes 48 | tf_op jit(solution)/shard_map/ppermute | solution.py:13
  13.9 0.7 fusion.45
  15.8 0.0 collective-permute-done.1
  15.9 3.5 %collective-permute-start.2 = (f32[3,32,1024]{2,1,0:T(8,128)S(1)}, f32[3,32,1024]{2,1,0:T(8,128)S(1)}, u32[]{:S(2)}, u32[]{:S(2)}) collective-permute-start(f32[3,32,1024]{2,1,0:T(8,128)S(1)} %constant_dynamic-slice_fusion.3), channel_id=1, source_target_pairs={{15,0},{0,1},{1,2},{2,3},{3,4},{4,5},{5,6},{6,7},{7,8},{8,9},{9,10... | collective-permute-start | bytes 1179656 | tf_op jit(solution)/shard_map/ppermute | solution.py:13
  22.5 0.6 broadcast_in_dim.72
  23.1 6.1 %all-to-all-start = ((s32[16,1,1]{2,1,0:T(1,128)}), s32[16,1,1]{2,1,0:T(1,128)S(1)}, u32[]{:S(2)}, u32[]{:S(2)}) async-start(s32[16,1,1]{2,1,0:T(1,128)} %broadcast_in_dim.72), calls=%async_computation | async-start | bytes 16384 | tf_op jit(solution)/shard_map/all_to_all | solution.py:18
  29.2 0.0 collective-permute-done.2
  29.3 2.8 %collective-permute-start.3 = (f32[3,32,1024]{2,1,0:T(8,128)S(1)}, f32[3,32,1024]{2,1,0:T(8,128)S(1)}, u32[]{:S(2)}, u32[]{:S(2)}) collective-permute-start(f32[3,32,1024]{2,1,0:T(8,128)S(1)} %constant_dynamic-slice_fusion.2), channel_id=1, source_target_pairs={{15,0},{0,1},{1,2},{2,3},{3,4},{4,5},{5,6},{6,7},{7,8},{8,9},{9,10... | collective-permute-start | bytes 1179656 | tf_op jit(solution)/shard_map/ppermute | solution.py:13
  32.1 0.3 all-to-all-done
  32.4 0.4 reduce.2
  32.8 0.1 slice.82
  32.9 0.1 slice.83
  33.0 0.1 slice.84
  33.1 0.1 slice.85
  33.2 0.1 slice.86
  33.3 0.1 slice.87
  33.4 0.6 fusion.44
  35.2 3.1 %collective-permute-done.3 = f32[3,32,1024]{2,1,0:T(8,128)S(1)} collective-permute-done((f32[3,32,1024]{2,1,0:T(8,128)S(1)}, f32[3,32,1024]{2,1,0:T(8,128)S(1)}, u32[]{:S(2)}, u32[]{:S(2)}) %collective-permute-start.3) | collective-permute-done | bytes 393248 | tf_op jit(solution)/shard_map/ppermute | solution.py:13
  38.4 5.6 %collective-permute-start.4 = (f32[3,32,1024]{2,1,0:T(8,128)S(1)}, f32[3,32,1024]{2,1,0:T(8,128)S(1)}, u32[]{:S(2)}, u32[]{:S(2)}) collective-permute-start(f32[3,32,1024]{2,1,0:T(8,128)S(1)} %constant_dynamic-slice_fusion.1), channel_id=1, source_target_pairs={{15,0},{0,1},{1,2},{2,3},{3,4},{4,5},{5,6},{6,7},{7,8},{8,9},{9,10... | collective-permute-start | bytes 1179656 | tf_op jit(solution)/shard_map/ppermute | solution.py:13
  44.0 0.0 copy-done
  44.0 0.2 select_reduce_fusion
  44.2 5.1 %collective-permute-done.4 = f32[3,32,1024]{2,1,0:T(8,128)S(1)} collective-permute-done((f32[3,32,1024]{2,1,0:T(8,128)S(1)}, f32[3,32,1024]{2,1,0:T(8,128)S(1)}, u32[]{:S(2)}, u32[]{:S(2)}) %collective-permute-start.4) | collective-permute-done | bytes 393248 | tf_op jit(solution)/shard_map/ppermute | solution.py:13
  49.3 0.1 slice.90
  49.5 13.7 %collective-permute-start.5 = (f32[1024]{0:T(1024)S(1)}, f32[1024]{0:T(1024)S(1)}, u32[]{:S(2)}, u32[]{:S(2)}) collective-permute-start(f32[1024]{0:T(1024)S(1)} %bitcast.38), channel_id=1, source_target_pairs={{0,1},{1,2},{2,3},{3,4},{4,5},{5,6},{6,7},{7,8},{8,9},{9,10},{10,1... | collective-permute-start | bytes 12296 | tf_op jit(solution)/shard_map/ppermute | solution.py:44
  63.2 0.1 slice_reduce_fusion.1
  63.3 2.6 %copy.29 = f32[8,32,1024]{1,2,0:T(8,128)} copy(f32[8,32,1024]{2,1,0:T(8,128)S(1)} %slice.90) | data formatting | bytes 2097152 | tf_op jit(solution)/shard_map/slice | solution.py:102
  66.0 0.1 concatenate.34
  66.1 0.1 concatenate.37
  66.2 2.1 %collective-permute-start.6 = (f32[1024]{0:T(1024)S(1)}, f32[1024]{0:T(1024)S(1)}, u32[]{:S(2)}, u32[]{:S(2)}) collective-permute-start(f32[1024]{0:T(1024)S(1)} %bitcast.39), channel_id=1, source_target_pairs={{1,0},{2,1},{3,2},{4,3},{5,4},{6,5},{7,6},{8,7},{9,8},{10,9},{11,1... | collective-permute-start | bytes 12296 | tf_op jit(solution)/shard_map/ppermute | solution.py:44
  68.3 0.0 collective-permute-done.5
  68.3 0.1 concatenate.33
  68.4 3.0 %copy.30 = f32[8,1,32,32]{1,3,2,0:T(8,128)} copy(f32[8,1,32,32]{3,2,1,0:T(8,128)S(1)} %pad_maximum_fusion) | data formatting | bytes 65536 | tf_op jit(solution)/shard_map/concatenate | solution.py:77
  71.4 5.1 %collective-permute-done.6 = f32[1024]{0:T(1024)S(1)} collective-permute-done((f32[1024]{0:T(1024)S(1)}, f32[1024]{0:T(1024)S(1)}, u32[]{:S(2)}, u32[]{:S(2)}) %collective-permute-start.6) | collective-permute-done | bytes 4128 | tf_op jit(solution)/shard_map/ppermute | solution.py:44
  76.5 0.1 broadcast_in_dim.70
  76.6 0.1 concatenate.38
  76.7 0.1 maximum_select_fusion
  76.7 3.0 %copy.31 = f32[8,1,32,32]{1,3,2,0:T(8,128)} copy(f32[8,1,32,32]{3,2,1,0:T(8,128)S(1)} %maximum_select_fusion) | data formatting | bytes 65536 | tf_op jit(solution)/shard_map/jit(_where)/select_n | solution.py:79
  79.7 9.0 %fusion.8 = f32[8,64,32,32]{1,3,2,0:T(8,128)} fusion(f32[8,1,32,32]{1,3,2,0:T(8,128)} %copy.31, f32[8,32,32,32]{1,3,2,0:T(8,128)} %bitcast.37, f32[8,1,32,32]{1,3,2,0:T(8,128)} %copy.30, s32[64]{0:T(128)S(1)} %get-tuple-element.19, s32[64]{0:T(128)S(1)} %get-tuple-element.20), kind=kOutput, calls=%fused_computation.9 | convolution fusion | flops 214477440 | bytes 3211776 | tf_op jit(solution)/shard_map/fx,pxyz->pfyz/dot_general | solution.py:61
  88.8 9.2 %copy.32 = f32[8,64,32,32]{2,3,1,0:T(8,128)} copy(f32[8,64,32,32]{1,3,2,0:T(8,128)} %fusion.8) | data formatting | bytes 4194304 | tf_op jit(solution)/shard_map/fx,pxyz->pfyz/transpose | solution.py:61
  97.9 9.0 %fusion.16 = f32[8,64,32,64]{3,2,1,0:T(8,128)S(1)} fusion(f32[8,64,32,32]{2,3,1,0:T(8,128)} %copy.32, s32[64]{0:T(128)S(1)} %get-tuple-element.18, s32[64]{0:T(128)S(1)} %get-tuple-element.17), kind=kOutput, calls=%fused_computation.24 | convolution fusion | flops 402663424 | bytes 6291968 | tf_op jit(solution)/shard_map/gy,pfyz->pfgz/dot_general | solution.py:62
  107.0 29.5 %fusion = f32[8,64,64,64]{3,2,1,0:T(8,128)} fusion(f32[8,64,32,64]{3,2,1,0:T(8,128)S(1)} %fusion.16, s32[64]{0:T(128)S(1)} %get-tuple-element.18, s32[64]{0:T(128)S(1)} %get-tuple-element.17), kind=kOutput, calls=%fused_computation | convolution fusion | flops 805316608 | bytes 12583424 | tf_op jit(solution)/shard_map/hz,pfgz->pfgh/dot_general | solution.py:63
  136.5 14.8 %reshape.174 = f32[8,64,4096]{2,1,0:T(8,128)} reshape(f32[8,64,64,64]{3,2,1,0:T(8,128)} %fusion) | data formatting | bytes 16777216 | tf_op jit(solution)/shard_map/reshape | solution.py:64
  151.2 6.5 %select_convert_fusion = bf16[8,64,4096]{2,1,0:T(8,128)(2,1)} fusion(f32[8,64,4096]{2,1,0:T(8,128)} %reshape.174, f32[8]{0:T(128)S(1)} %multiply_add_fusion, pred[8]{0:T(512)(128)(4,1)S(1)} %iota_compare_fusion.12), kind=kLoop, calls=%fused_computation.2 | loop fusion | flops 6291456 | bytes 12582952 | tf_op jit(solution)/shard_map/convert_element_type | solution.py:83
  (20 shorter events, 0.3 us)
Async XLA Ops:
  2.7 41.3 %copy-start = (s32[1,128]{1,0:T(1,128)S(1)}, s32[1,128]{1,0:T(1,128)}, u32[]{:S(2)}) copy-start(s32[1,128]{1,0:T(1,128)} %param.7) | copy-start | bytes 1540
  3.7 12.1 %collective-permute-start.1 = (f32[3,32,1024]{2,1,0:T(8,128)S(1)}, f32[3,32,1024]{2,1,0:T(8,128)S(1)}, u32[]{:S(2)}, u32[]{:S(2)}) collective-permute-start(f32[3,32,1024]{2,1,0:T(8,128)S(1)} %pad_dynamic-slice_fusion), channel_id=1, source_target_pairs={{15,0},{0,1},{1,2},{2,3},{3,4},{4,5},{5,6},{6,7},{7,8},{8,9},{9,10... | collective-permute-start | bytes 1179656 | tf_op jit(solution)/shard_map/ppermute | solution.py:13
  3.8 10.0 %collective-permute-start = (s32[1,4]{1,0:T(1,128)}, s32[1,4]{1,0:T(1,128)S(1)}, u32[]{:S(2)}, u32[]{:S(2)}) collective-permute-start(s32[1,4]{1,0:T(1,128)} %param.6), channel_id=1, source_target_pairs={{15,0},{0,1},{1,2},{2,3},{3,4},{4,5},{5,6},{6,7},{7,8},{8,9},{9,10... | collective-permute-start | bytes 56 | tf_op jit(solution)/shard_map/ppermute | solution.py:13
  15.9 13.3 %collective-permute-start.2 = (f32[3,32,1024]{2,1,0:T(8,128)S(1)}, f32[3,32,1024]{2,1,0:T(8,128)S(1)}, u32[]{:S(2)}, u32[]{:S(2)}) collective-permute-start(f32[3,32,1024]{2,1,0:T(8,128)S(1)} %constant_dynamic-slice_fusion.3), channel_id=1, source_target_pairs={{15,0},{0,1},{1,2},{2,3},{3,4},{4,5},{5,6},{6,7},{7,8},{8,9},{9,10... | collective-permute-start | bytes 1179656 | tf_op jit(solution)/shard_map/ppermute | solution.py:13
  23.1 9.2 %all-to-all-start = ((s32[16,1,1]{2,1,0:T(1,128)}), s32[16,1,1]{2,1,0:T(1,128)S(1)}, u32[]{:S(2)}, u32[]{:S(2)}) async-start(s32[16,1,1]{2,1,0:T(1,128)} %broadcast_in_dim.72), calls=%async_computation | async-start | bytes 16384 | tf_op jit(solution)/shard_map/all_to_all | solution.py:18
  29.3 9.0 %collective-permute-start.3 = (f32[3,32,1024]{2,1,0:T(8,128)S(1)}, f32[3,32,1024]{2,1,0:T(8,128)S(1)}, u32[]{:S(2)}, u32[]{:S(2)}) collective-permute-start(f32[3,32,1024]{2,1,0:T(8,128)S(1)} %constant_dynamic-slice_fusion.2), channel_id=1, source_target_pairs={{15,0},{0,1},{1,2},{2,3},{3,4},{4,5},{5,6},{6,7},{7,8},{8,9},{9,10... | collective-permute-start | bytes 1179656 | tf_op jit(solution)/shard_map/ppermute | solution.py:13
  38.4 10.9 %collective-permute-start.4 = (f32[3,32,1024]{2,1,0:T(8,128)S(1)}, f32[3,32,1024]{2,1,0:T(8,128)S(1)}, u32[]{:S(2)}, u32[]{:S(2)}) collective-permute-start(f32[3,32,1024]{2,1,0:T(8,128)S(1)} %constant_dynamic-slice_fusion.1), channel_id=1, source_target_pairs={{15,0},{0,1},{1,2},{2,3},{3,4},{4,5},{5,6},{6,7},{7,8},{8,9},{9,10... | collective-permute-start | bytes 1179656 | tf_op jit(solution)/shard_map/ppermute | solution.py:13
  49.5 18.8 %collective-permute-start.5 = (f32[1024]{0:T(1024)S(1)}, f32[1024]{0:T(1024)S(1)}, u32[]{:S(2)}, u32[]{:S(2)}) collective-permute-start(f32[1024]{0:T(1024)S(1)} %bitcast.38), channel_id=1, source_target_pairs={{0,1},{1,2},{2,3},{3,4},{4,5},{5,6},{6,7},{7,8},{8,9},{9,10},{10,1... | collective-permute-start | bytes 12296 | tf_op jit(solution)/shard_map/ppermute | solution.py:44
  66.2 10.4 %collective-permute-start.6 = (f32[1024]{0:T(1024)S(1)}, f32[1024]{0:T(1024)S(1)}, u32[]{:S(2)}, u32[]{:S(2)}) collective-permute-start(f32[1024]{0:T(1024)S(1)} %bitcast.39), channel_id=1, source_target_pairs={{1,0},{2,1},{3,2},{4,3},{5,4},{6,5},{7,6},{8,7},{9,8},{10,9},{11,1... | collective-permute-start | bytes 12296 | tf_op jit(solution)/shard_map/ppermute | solution.py:44
where the time goes:
time: 159 us; the launch traced here: 158 us
  matrix products  47.5 us (30%)
  local copies, waits for them, and re-layouts  39.8 us (25%)
  starting transfers between devices  35 us (22%)
  waiting for transfers between devices  21.1 us (13%)
  other arithmetic  7.25 us (5%)
  between operations  7.1 us (4%)
    dot_general x1, matrix products, refine(): third = jnp.einsum('hz,pfgz->pfgh', inner, second, precision=highest)  29.5 us
    ppermute x2, starting transfers between devices, from_behind(): return lax.ppermute(x, axis, pairs)  15.8 us
    ppermute x5, waiting for transfers between devices, passed_along(): return lax.ppermute(block, axis, route)  15.7 us
    reshape x1, local copies, waits for them, and re-layouts, refine(): return third.reshape(number, 2 * edge, 4 * edge * edge)  14.8 us
    ppermute x5, starting transfers between devices, passed_along(): return lax.ppermute(block, axis, route)  13.1 us
    transpose x1, local copies, waits for them, and re-layouts, refine(): first = jnp.einsum('fx,pxyz->pfyz', across, cube, precision=highest)  9.17 us
    dot_general x1, matrix products, refine(): second = jnp.einsum('gy,pfyz->pfgz', inner, first, precision=highest)  9.04 us
    dot_general x1, matrix products, refine(): first = jnp.einsum('fx,pxyz->pfyz', across, cube, precision=highest)  9.03 us
  transfers between devices with their start and end apart: 8, of which 5 were waited for; matrix products, arithmetic and copies ran while one was open for 7% of the time, Pallas kernels for 0%

commit v1 on v0

--- a/solution.py
+++ b/solution.py
@@ -1,6 +1,9 @@
 import jax
 import jax.numpy as jnp
+import numpy as np
 from jax import lax
+from jax.experimental import pallas as pl
+from jax.experimental.pallas import tpu as pltpu
 from jax.sharding import PartitionSpec as P
 
 MOST = 3
@@ -44,43 +47,80 @@
     return lax.ppermute(x, axis, pairs)
 
 
-def refine_table(edge, margin):
-    finer = jnp.arange(2 * edge)[:, None]
-    coarse = jnp.arange(edge + 2 * margin)[None, :]
-    home = finer // 2 + margin
-    side = home + 2 * (finer % 2) - 1
-    return (0.75 * (coarse == home) + 0.25 * (coarse == side)).astype(jnp.float32)
+def refine_weights():
+    fine = np.arange(64)
+    home, side = fine // 2, fine // 2 + 2 * (fine % 2) - 1
+    grid = np.arange(32)[:, None]
+    z = 0.75 * (grid == home) + 0.25 * (grid == side)
+    y = np.zeros((4, 2, 2), np.float32)
+    for c in range(2):
+        y[c + 1, c, :] = 0.75
+        y[c, c, 0] = 0.25
+        y[c + 2, c, 1] = 0.25
+    half = np.kron(y.reshape(4, 4), z)
+    return np.concatenate([half, half], 0)
 
+def refine_kernel(info, tags, field, lower, upper, weights, fine, rows, stage, done, in_sem, out_sem):
+    slots, edge = field.shape[0], field.shape[1]
+    loads = [pltpu.make_async_copy(field.at[j], rows.at[pl.ds(8 + edge * j, edge)], in_sem.at[j]) for j in range(slots)]
+    for load in loads:
+        load.start()
+    live, offset = info[0], info[1]
+    for load in loads:
+        load.wait()
+    rows[pl.ds(7, 1), :] = jnp.where(info[2] == 0, 0.0, lower[...])
+    rows[pl.ds(8 + edge * live, 1), :] = jnp.where(info[3] == 0, 0.0, upper[...])
+    lanes = lax.broadcasted_iota(jnp.int32, (2 * edge, 128), 1)
+    zeros = jnp.zeros((2 * edge, 128), jnp.float32)
 
-def refine(extended, edge):
-    number = extended.shape[0]
-    cube = extended.reshape(number, edge + 2, edge, edge)
-    across = refine_table(edge, 1)
-    inner = refine_table(edge, 0)
-    highest = lax.Precision.HIGHEST
-    first = jnp.einsum("fx,pxyz->pfyz", across, cube, precision=highest)
-    second = jnp.einsum("gy,pfyz->pfgz", inner, first, precision=highest)
-    third = jnp.einsum("hz,pfgz->pfgh", inner, second, precision=highest)
-    return third.reshape(number, 2 * edge, 4 * edge * edge)
+    def one(j, carry):
+        start = pl.multiple_of(edge * j, 8)
+        tag = tags[0, jnp.minimum(offset + j, tags.shape[1] - 1)]
+        factor = jnp.where(j < live, 1.0 + 0.5 * tag.astype(jnp.float32), 0.0)
+        for m in range(8):
+            part = rows[pl.ds(start, edge + 16), pl.ds(128 * m, 128)] * factor
+            home = 0.75 * part[8:8 + edge]
+            quarter = 0.25 * part
+            stage[m, pl.ds(0, edge, stride=2), :] = home + quarter[7:7 + edge]
+            stage[m, pl.ds(1, edge, stride=2), :] = home + quarter[9:9 + edge]
+        def emit(window, value):
+            high = value.astype(jnp.bfloat16)
+            low = (value - high.astype(jnp.float32)).astype(jnp.bfloat16)
+            both = jnp.concatenate([high, low], axis=1)
+            got = jnp.dot(both, weights[...], preferred_element_type=jnp.float32)
+            done[j, :, pl.ds(256 * window, 256)] = got.astype(jnp.bfloat16)
+        right_before = zeros
+        tile = stage[0]
+        left = pltpu.roll(tile, 96, 1)
+        for m in range(8):
+            right = pltpu.roll(tile, 32, 1)
+            emit(2 * m, jnp.where(lanes < 32, right_before, right))
+            right_before = right
+            if m < 7:
+                tile = stage[m + 1]
+                left_next = pltpu.roll(tile, 96, 1)
+            else:
+                left_next = zeros
+            emit(2 * m + 1, jnp.where(lanes < 96, left, left_next))
+            left = left_next
+        pltpu.make_async_copy(done.at[j], fine.at[j], out_sem.at[j]).start()
+        return carry
 
+    lax.fori_loop(0, slots, one, 0)
+    for j in range(slots):
+        pltpu.make_async_copy(done.at[j], fine.at[j], out_sem.at[j]).wait()
 
-def tag_factors(tag_row, offset, capacity):
-    position = offset + jnp.arange(capacity)
-    boxes = jnp.arange(tag_row.shape[0])
-    picked = jnp.sum(jnp.where(position[:, None] == boxes[None, :], tag_row[None, :], 0), axis=1)
-    return 1.0 + 0.5 * picked.astype(jnp.float32)
-
-
-def finish(work, live, lower, upper, factors):
-    capacity, edge = (work.shape[0], work.shape[1])
-    slots = jnp.arange(capacity)
-    below = jnp.concatenate([lower[None], work[:-1, edge - 1]], 0)
-    above = jnp.concatenate([work[1:, 0], upper[None]], 0)
-    above = jnp.where((slots == live - 1)[:, None], upper[None], above)
-    extended = jnp.concatenate([below[:, None], work, above[:, None]], 1)
-    refined = refine(extended, edge)
-    scaled = refined * factors[:, None, None]
-    return jnp.where((slots < live)[:, None, None], scaled, 0.0).astype(jnp.bfloat16)
+def refine(info, tags, field, lower, upper, weights):
+    return pl.pallas_call(
+        refine_kernel,
+        out_shape=jax.ShapeDtypeStruct((8, 64, 4096), jnp.bfloat16),
+        in_specs=[pl.BlockSpec(memory_space=pltpu.SMEM)] * 2 + [pl.BlockSpec(memory_space=pl.ANY)] + [pl.BlockSpec(memory_space=pltpu.VMEM)] * 3,
+        out_specs=pl.BlockSpec(memory_space=pl.ANY),
+        scratch_shapes=[pltpu.VMEM((272, 1024), jnp.float32), pltpu.VMEM((8, 64, 128), jnp.float32),
+                        pltpu.VMEM((8, 64, 4096), jnp.bfloat16),
+                        pltpu.SemaphoreType.DMA((8,)), pltpu.SemaphoreType.DMA((8,))],
+        name="refine",
+    )(info, tags, field, lower, upper, weights)
 
 
 def add_counts(earlier, later):
@@ -104,7 +144,11 @@
     top_patch = lax.dynamic_index_in_dim(work, live - 1, 0, keepdims=False)
     lower = from_behind(top_patch[edge - 1], ("grp", "blk"), 1)
     upper = from_behind(work[0, 0], ("grp", "blk"), -1)
-    return finish(work, live, lower, upper, tag_factors(tags[0], offset, capacity))
+    place = lax.axis_index("grp") * lax.axis_size("blk") + lax.axis_index("blk")
+    last = lax.axis_size("grp") * lax.axis_size("blk") - 1
+    info = jnp.stack([live, offset, (place > 0).astype(jnp.int32), (place < last).astype(jnp.int32)])
+    weights = jnp.asarray(refine_weights(), jnp.bfloat16)
+    return refine(info, tags, work, lower[None], upper[None], weights)
 
 
 def solution(mesh):

time: 159 us -> 89 us (0.56)
  matrix products: 47.5 us -> 0 us
  local copies, waits for them, and re-layouts: 39.8 us -> 6.03 us
  waiting for transfers between devices: 21.1 us -> 30.4 us
  Pallas kernels: 0 us -> 7.56 us
  other arithmetic: 7.25 us -> 1.06 us
    dot_general x3 -> x0, matrix products: 47.5 us -> none  [the longest x1 29.5 us: refine(): third = jnp.einsum('hz,pfgz->pfgh', inner, second, precision=highest)]
    reshape x1 -> x0, local copies, waits for them, and re-layouts: 14.8 us -> none  [refine(): return third.reshape(number, 2 * edge, 4 * edge * edge)]
    transpose x1 -> x0, local copies, waits for them, and re-layouts: 9.17 us -> none  [refine(): first = jnp.einsum('fx,pxyz->pfyz', across, cube, precision=highest)]
    pallas_call x0 -> x1, Pallas kernels: none -> 7.56 us  [refine(): pl.pallas_call(refine_kernel, out_shape=jax.ShapeDtypeStruct((8, 64, 4096...]
    convert_element_type x1 -> x0, other arithmetic: 6.54 us -> none  [finish(): jnp.where((slots < live)[:, None, None], scaled, 0.0).astype(jnp.bfloat16)]
    ppermute x5, waiting for transfers between devices: 15.7 us -> 19.4 us  [passed_along(): return lax.ppermute(block, axis, route)]
    concatenate x5 -> x0, local copies, waits for them, and re-layouts: 3.34 us -> none  [the longest x3 3.18 us: finish(): below = jnp.concatenate([lower[None], work[:-1, edge - 1]], 0)]
    select_n x1 -> x0, local copies, waits for them, and re-layouts: 3 us -> none  [finish(): above = jnp.where((slots == live - 1)[:, None], upper[None], above)]
  transfers between devices with their start and end apart: 8 -> 8, of which waited for: 5 -> 5; matrix products, arithmetic and copies ran while one was open for 7% -> 4% of each run, Pallas kernels for 0% -> 0%
where the time goes in v1:
time: 89 us; the launch traced here: 88.5 us
  starting transfers between devices  36.3 us (41%)
  waiting for transfers between devices  30.4 us (34%)
  Pallas kernels  7.56 us (8%)
  between operations  7.25 us (8%)
  local copies, waits for them, and re-layouts  6.03 us (7%)
  other arithmetic  1.06 us (1%)
    ppermute x5, waiting for transfers between devices, passed_along(): return lax.ppermute(block, axis, route)  19.4 us
    ppermute x5, starting transfers between devices, passed_along(): return lax.ppermute(block, axis, route)  15.9 us
    ppermute x2, starting transfers between devices, from_behind(): return lax.ppermute(x, axis, pairs)  14.3 us
    ppermute x2, waiting for transfers between devices, from_behind(): return lax.ppermute(x, axis, pairs)  7.77 us
    pallas_call x1, Pallas kernels, refine(): pl.pallas_call(refine_kernel, out_shape=jax.ShapeDtypeStruct((8, 64, 4096...  7.56 us
    all_to_all x1, starting transfers between devices, from_everyone(): lax.all_to_all(jnp.broadcast_to(x[None], (devices, *x.shape)), axis, 0, 0...  6.08 us
    all_to_all x1, waiting for transfers between devices, from_everyone(): lax.all_to_all(jnp.broadcast_to(x[None], (devices, *x.shape)), axis, 0, 0...  3.16 us
  transfers between devices with their start and end apart: 8, of which 5 were waited for; matrix products, arithmetic and copies ran while one was open for 4% of the time, Pallas kernels for 0%

profile of v1, /device:TPU:127, one launch (start us, length us, event | category | flops | bytes accessed | tf_op | source)
XLA Modules:
  0.0 88.5 jit_solution(424715971587379391)
XLA Ops:
  0.0 0.0 copy-start.2
  0.0 0.0 copy-start.1
  0.7 1.5 %fusion.2 = (s32[1,1]{1,0:T(1,128)}, s32[1,1]{1,0:T(1,128)}, s32[1,1]{1,0:T(1,128)}, s32[1,1]{1,0:T(1,128)}) fusion(s32[1,4]{1,0:T(1,128)} %param.7), kind=kLoop, calls=%fused_computation.13 | loop fusion | bytes 32 | tf_op jit(solution)/shard_map/slice | solution.py:137
  2.8 1.0 %pad_dynamic-slice_fusion = f32[3,32,1024]{2,1,0:T(8,128)S(1)} fusion(s32[]{:T(128)S(6)} %select_n.33, f32[8,32,1024]{2,1,0:T(8,128)} %param.5), kind=kLoop, calls=%fused_computation | loop fusion | bytes 1441796 | tf_op jit(solution)/shard_map/dynamic_slice | solution.py:138
  3.8 0.1 collective-permute-start.1
  3.9 0.0 copy-done.2
  3.9 1.1 %collective-permute-start = (s32[1,4]{1,0:T(1,128)S(1)}, s32[1,4]{1,0:T(1,128)S(1)}, u32[]{:S(2)}, u32[]{:S(2)}) collective-permute-start(s32[1,4]{1,0:T(1,128)S(1)} %copy-done.2), channel_id=1, source_target_pairs={{15,0},{0,1},{1,2},{2,3},{3,4},{4,5},{5,6},{6,7},{7,8},{8,9},{9,10... | collective-permute-start | bytes 56 | tf_op jit(solution)/shard_map/ppermute | solution.py:16
  5.0 0.0 copy-done.1
  5.0 0.1 concatenate.3
  5.2 8.8 %collective-permute-done = s32[1,4]{1,0:T(1,128)S(1)} collective-permute-done((s32[1,4]{1,0:T(1,128)S(1)}, s32[1,4]{1,0:T(1,128)S(1)}, u32[]{:S(2)}, u32[]{:S(2)}) %collective-permute-start) | collective-permute-done | bytes 48 | tf_op jit(solution)/shard_map/ppermute | solution.py:16
  14.0 0.7 fusion.1
  16.0 0.0 collective-permute-done.1
  16.1 3.5 %collective-permute-start.2 = (f32[3,32,1024]{2,1,0:T(8,128)S(1)}, f32[3,32,1024]{2,1,0:T(8,128)S(1)}, u32[]{:S(2)}, u32[]{:S(2)}) collective-permute-start(f32[3,32,1024]{2,1,0:T(8,128)S(1)} %constant_dynamic-slice_fusion.3), channel_id=1, source_target_pairs={{15,0},{0,1},{1,2},{2,3},{3,4},{4,5},{5,6},{6,7},{7,8},{8,9},{9,10... | collective-permute-start | bytes 1179656 | tf_op jit(solution)/shard_map/ppermute | solution.py:16
  20.8 5.7 %collective-permute-done.2 = f32[3,32,1024]{2,1,0:T(8,128)S(1)} collective-permute-done((f32[3,32,1024]{2,1,0:T(8,128)S(1)}, f32[3,32,1024]{2,1,0:T(8,128)S(1)}, u32[]{:S(2)}, u32[]{:S(2)}) %collective-permute-start.2) | collective-permute-done | bytes 393248 | tf_op jit(solution)/shard_map/ppermute | solution.py:16
  26.6 5.6 %collective-permute-start.3 = (f32[3,32,1024]{2,1,0:T(8,128)S(1)}, f32[3,32,1024]{2,1,0:T(8,128)S(1)}, u32[]{:S(2)}, u32[]{:S(2)}) collective-permute-start(f32[3,32,1024]{2,1,0:T(8,128)S(1)} %constant_dynamic-slice_fusion.2), channel_id=1, source_target_pairs={{15,0},{0,1},{1,2},{2,3},{3,4},{4,5},{5,6},{6,7},{7,8},{8,9},{9,10... | collective-permute-start | bytes 1179656 | tf_op jit(solution)/shard_map/ppermute | solution.py:16
  33.4 5.0 %collective-permute-done.3 = f32[3,32,1024]{2,1,0:T(8,128)S(1)} collective-permute-done((f32[3,32,1024]{2,1,0:T(8,128)S(1)}, f32[3,32,1024]{2,1,0:T(8,128)S(1)}, u32[]{:S(2)}, u32[]{:S(2)}) %collective-permute-start.3) | collective-permute-done | bytes 393248 | tf_op jit(solution)/shard_map/ppermute | solution.py:16
  38.4 5.6 %collective-permute-start.4 = (f32[3,32,1024]{2,1,0:T(8,128)S(1)}, f32[3,32,1024]{2,1,0:T(8,128)S(1)}, u32[]{:S(2)}, u32[]{:S(2)}) collective-permute-start(f32[3,32,1024]{2,1,0:T(8,128)S(1)} %constant_dynamic-slice_fusion.1), channel_id=1, source_target_pairs={{15,0},{0,1},{1,2},{2,3},{3,4},{4,5},{5,6},{6,7},{7,8},{8,9},{9,10... | collective-permute-start | bytes 1179656 | tf_op jit(solution)/shard_map/ppermute | solution.py:16
  44.7 0.6 broadcast_in_dim.16
  45.3 6.1 %all-to-all-start = ((s32[16,1,1]{2,1,0:T(1,128)}), s32[16,1,1]{2,1,0:T(1,128)S(1)}, u32[]{:S(2)}, u32[]{:S(2)}) async-start(s32[16,1,1]{2,1,0:T(1,128)} %broadcast_in_dim.16), calls=%async_computation | async-start | bytes 16384 | tf_op jit(solution)/shard_map/all_to_all | solution.py:21
  51.4 3.2 %all-to-all-done = s32[16,1,1]{2,1,0:T(1,128)S(1)} async-done(((s32[16,1,1]{2,1,0:T(1,128)}), s32[16,1,1]{2,1,0:T(1,128)S(1)}, u32[]{:S(2)}, u32[]{:S(2)}) %all-to-all-start) | async-done | bytes 96 | tf_op jit(solution)/shard_map/all_to_all | solution.py:21
  54.5 0.4 reduce
  54.9 0.1 slice.70
  55.0 0.1 slice.69
  55.1 0.1 slice.72
  55.2 0.1 slice.71
  55.3 0.1 slice.74
  55.4 0.1 slice.73
  55.5 0.6 fusion
  57.4 0.0 collective-permute-done.4
  57.5 0.1 slice.80.field
  57.6 0.0 copy-start
  57.6 12.4 %collective-permute-start.5 = (f32[1024]{0:T(1024)S(1)}, f32[1024]{0:T(1024)S(1)}, u32[]{:S(2)}, u32[]{:S(2)}) collective-permute-start(f32[1024]{0:T(1024)S(1)} %bitcast.21), channel_id=1, source_target_pairs={{0,1},{1,2},{2,3},{3,4},{4,5},{5,6},{6,7},{7,8},{8,9},{9,10},{10,1... | collective-permute-start | bytes 12296 | tf_op jit(solution)/shard_map/ppermute | solution.py:47
  70.0 1.9 %collective-permute-start.6 = (f32[1024]{0:T(1024)S(1)}, f32[1024]{0:T(1024)S(1)}, u32[]{:S(2)}, u32[]{:S(2)}) collective-permute-start(f32[1024]{0:T(1024)S(1)} %bitcast.20), channel_id=1, source_target_pairs={{1,0},{2,1},{3,2},{4,3},{5,4},{6,5},{7,6},{8,7},{9,8},{10,9},{11,1... | collective-permute-start | bytes 12296 | tf_op jit(solution)/shard_map/ppermute | solution.py:47
  72.0 0.7 pad_add_fusion.info
  72.6 0.0 collective-permute-done.5
  72.6 0.0 copy-start.3
  72.6 7.8 %collective-permute-done.6 = f32[1024]{0:T(1024)S(1)} collective-permute-done((f32[1024]{0:T(1024)S(1)}, f32[1024]{0:T(1024)S(1)}, u32[]{:S(2)}, u32[]{:S(2)}) %collective-permute-start.6) | collective-permute-done | bytes 4128 | tf_op jit(solution)/shard_map/ppermute | solution.py:47
  80.4 0.0 copy-start.4
  80.4 0.0 copy-done
  80.4 0.0 copy-done.3
  80.4 0.6 copy-done.4
  81.0 7.6 %refine.1 = bf16[8,64,4096]{2,1,0:T(8,128)(2,1)} custom-call(s32[4]{0:T(128)} %pad_add_fusion.info, s32[1,128]{1,0:T(1,128)} %tags.1, f32[8,32,1024]{2,1,0:T(8,128)} %copy-done, f32[1,1024]{1,0:T(1,128)} %bitcast.22, f32[1,1024]{1,0:T(1,128)} %bitcast.23, bf16[256,256]{1,0:T(8,128)(2,1)} %constant.30.clone.weights), custom_call_target="tpu_custom_call" | custom-call | tf_op jit(solution)/shard_map/refine/pallas_call | solution.py:114
  (13 shorter events, 0.3 us)
Async XLA Ops:
  0.0 3.9 %copy-start.2 = (s32[1,4]{1,0:T(1,128)S(1)}, s32[1,4]{1,0:T(1,128)}, u32[]{:S(2)}) copy-start(s32[1,4]{1,0:T(1,128)} %param.7) | copy-start | bytes 52
  0.0 5.0 %copy-start.1 = (f32[8,32,1024]{2,1,0:T(8,128)S(1)}, f32[8,32,1024]{2,1,0:T(8,128)}, u32[]{:S(2)}) copy-start(f32[8,32,1024]{2,1,0:T(8,128)} %param.5) | copy-start | bytes 3145732
  3.8 12.2 %collective-permute-start.1 = (f32[3,32,1024]{2,1,0:T(8,128)S(1)}, f32[3,32,1024]{2,1,0:T(8,128)S(1)}, u32[]{:S(2)}, u32[]{:S(2)}) collective-permute-start(f32[3,32,1024]{2,1,0:T(8,128)S(1)} %pad_dynamic-slice_fusion), channel_id=1, source_target_pairs={{15,0},{0,1},{1,2},{2,3},{3,4},{4,5},{5,6},{6,7},{7,8},{8,9},{9,10... | collective-permute-start | bytes 1179656 | tf_op jit(solution)/shard_map/ppermute | solution.py:16
  3.9 10.1 %collective-permute-start = (s32[1,4]{1,0:T(1,128)S(1)}, s32[1,4]{1,0:T(1,128)S(1)}, u32[]{:S(2)}, u32[]{:S(2)}) collective-permute-start(s32[1,4]{1,0:T(1,128)S(1)} %copy-done.2), channel_id=1, source_target_pairs={{15,0},{0,1},{1,2},{2,3},{3,4},{4,5},{5,6},{6,7},{7,8},{8,9},{9,10... | collective-permute-start | bytes 56 | tf_op jit(solution)/shard_map/ppermute | solution.py:16
  16.1 10.5 %collective-permute-start.2 = (f32[3,32,1024]{2,1,0:T(8,128)S(1)}, f32[3,32,1024]{2,1,0:T(8,128)S(1)}, u32[]{:S(2)}, u32[]{:S(2)}) collective-permute-start(f32[3,32,1024]{2,1,0:T(8,128)S(1)} %constant_dynamic-slice_fusion.3), channel_id=1, source_target_pairs={{15,0},{0,1},{1,2},{2,3},{3,4},{4,5},{5,6},{6,7},{7,8},{8,9},{9,10... | collective-permute-start | bytes 1179656 | tf_op jit(solution)/shard_map/ppermute | solution.py:16
  26.6 11.7 %collective-permute-start.3 = (f32[3,32,1024]{2,1,0:T(8,128)S(1)}, f32[3,32,1024]{2,1,0:T(8,128)S(1)}, u32[]{:S(2)}, u32[]{:S(2)}) collective-permute-start(f32[3,32,1024]{2,1,0:T(8,128)S(1)} %constant_dynamic-slice_fusion.2), channel_id=1, source_target_pairs={{15,0},{0,1},{1,2},{2,3},{3,4},{4,5},{5,6},{6,7},{7,8},{8,9},{9,10... | collective-permute-start | bytes 1179656 | tf_op jit(solution)/shard_map/ppermute | solution.py:16
  38.4 19.0 %collective-permute-start.4 = (f32[3,32,1024]{2,1,0:T(8,128)S(1)}, f32[3,32,1024]{2,1,0:T(8,128)S(1)}, u32[]{:S(2)}, u32[]{:S(2)}) collective-permute-start(f32[3,32,1024]{2,1,0:T(8,128)S(1)} %constant_dynamic-slice_fusion.1), channel_id=1, source_target_pairs={{15,0},{0,1},{1,2},{2,3},{3,4},{4,5},{5,6},{6,7},{7,8},{8,9},{9,10... | collective-permute-start | bytes 1179656 | tf_op jit(solution)/shard_map/ppermute | solution.py:16
  45.3 9.2 %all-to-all-start = ((s32[16,1,1]{2,1,0:T(1,128)}), s32[16,1,1]{2,1,0:T(1,128)S(1)}, u32[]{:S(2)}, u32[]{:S(2)}) async-start(s32[16,1,1]{2,1,0:T(1,128)} %broadcast_in_dim.16), calls=%async_computation | async-start | bytes 16384 | tf_op jit(solution)/shard_map/all_to_all | solution.py:21
  57.6 22.8 %copy-start = (f32[8,32,1024]{2,1,0:T(8,128)}, f32[8,32,1024]{2,1,0:T(8,128)S(1)}, u32[]{:S(2)}) copy-start(f32[8,32,1024]{2,1,0:T(8,128)S(1)} %slice.80.field) | copy-start | bytes 3145732
  57.6 15.0 %collective-permute-start.5 = (f32[1024]{0:T(1024)S(1)}, f32[1024]{0:T(1024)S(1)}, u32[]{:S(2)}, u32[]{:S(2)}) collective-permute-start(f32[1024]{0:T(1024)S(1)} %bitcast.21), channel_id=1, source_target_pairs={{0,1},{1,2},{2,3},{3,4},{4,5},{5,6},{6,7},{7,8},{8,9},{9,10},{10,1... | collective-permute-start | bytes 12296 | tf_op jit(solution)/shard_map/ppermute | solution.py:47
  70.0 10.4 %collective-permute-start.6 = (f32[1024]{0:T(1024)S(1)}, f32[1024]{0:T(1024)S(1)}, u32[]{:S(2)}, u32[]{:S(2)}) collective-permute-start(f32[1024]{0:T(1024)S(1)} %bitcast.20), channel_id=1, source_target_pairs={{1,0},{2,1},{3,2},{4,3},{5,4},{6,5},{7,6},{8,7},{9,8},{10,9},{11,1... | collective-permute-start | bytes 12296 | tf_op jit(solution)/shard_map/ppermute | solution.py:47
  72.6 7.8 %copy-start.3 = (f32[1024]{0:T(1024)}, f32[1024]{0:T(1024)S(1)}, u32[]{:S(2)}) copy-start(f32[1024]{0:T(1024)S(1)} %collective-permute-done.5) | copy-start | bytes 12292
  80.4 0.6 copy-start.4

commit v2 on v1

v2 whole, which is shorter than its diff:
```python
import jax
import jax.numpy as jnp
import numpy as np
from jax import lax
from jax.experimental import pallas as pl
from jax.experimental.pallas import tpu as pltpu
from jax.sharding import PartitionSpec as P

MOST = 3
STEPS = 4
MESH = pl.DeviceIdType.MESH
SIDE = 4
CAP = 8
HELD = CAP - 1
OWN = SIDE * HELD
CROSS = MOST * STEPS
PARTS = 4
FAR = 1000

def exchange_kernel(counts, moves, patches, moved, planes, info, *scratch):
    scratch = list(scratch)
    def take(number):
        out = scratch[:number]
        del scratch[:number]
        return out
    pool, crossing_in, crossing_out, final = take(PARTS), take(PARTS), take(PARTS), take(PARTS)
    table, numbers, cuts, above, wanted, corner, edges, bases, tops = take(9)
    (pool_send, pool_recv, pool_local, cross_send, cross_recv, final_send, final_recv, final_local,
     meta_send, meta_recv, small, plane_send, plane_recv, base_send, base_recv, top_send) = scratch

    grp, blk = lax.axis_index("grp"), lax.axis_index("blk")
    groups, devices = lax.axis_size("grp"), lax.axis_size("blk")
    row, place = lax.div(blk, SIDE), lax.rem(blk, SIDE)
    rows_of_devices = devices // SIDE
    width = patches.shape[2] // PARTS
    depth = patches.shape[1] // SIDE
    line = grp * devices + blk
    after = lax.rem(line + 1, groups * devices)
    before = lax.rem(line + groups * devices - 1, groups * devices)
    after, before = [(lax.div(other, devices), lax.rem(other, devices)) for other in (after, before)]

    def across(k):
        return lax.rem(place + k, SIDE)

    def beside(k):
        return (grp, row * SIDE + across(k))

    def over(k):
        return (grp, lax.rem(row + k, rows_of_devices) * SIDE + place)

    def remote(src, dst, send, recv, device):
        return pltpu.make_async_remote_copy(src_ref=src, dst_ref=dst, send_sem=send, recv_sem=recv, device_id=device, device_id_type=MESH)

    def lanes(part):
        return pl.ds(width * part, width)

    def strip(home):
        return pl.ds(pl.multiple_of(home * depth, depth), depth)

    local = [pltpu.make_async_copy(patches.at[pl.ds(1, HELD), strip(place), lanes(i)], pool[i].at[pl.ds(HELD * place, HELD)], pool_local.at[i]) for i in range(PARTS)]
    ends = [pltpu.make_async_copy(patches.at[0, pl.ds(0, 8)], corner.at[0], small.at[0]),
            pltpu.make_async_copy(patches.at[0, pl.ds(patches.shape[1] - 8, 8)], corner.at[1], small.at[1])]
    for copy in ends + local:
        copy.start()
    lane = lax.broadcasted_iota(jnp.int32, (1, 128), 1)
    mine = jnp.where(lane == 0, counts[0], 0)
    for s in range(STEPS):
        mine = jnp.where(lane == 1 + s, moves[0, s], mine)
    table[blk] = mine

    barrier = pltpu.get_barrier_semaphore()
    for k in range(1, SIDE):
        pl.semaphore_signal(barrier, inc=1, device_id=beside(k), device_id_type=MESH)
    for k in range(1, rows_of_devices):
        pl.semaphore_signal(barrier, inc=1, device_id=over(k), device_id_type=MESH)
    first, last = place == 0, place == SIDE - 1
    @pl.when(last)
    def _():
        pl.semaphore_signal(barrier, inc=1, device_id=after, device_id_type=MESH)
    @pl.when(first)
    def _():
        pl.semaphore_signal(barrier, inc=1, device_id=before, device_id_type=MESH)
    pl.semaphore_wait(barrier, SIDE - 1 + rows_of_devices - 1 + jnp.where(first, 1, 0) + jnp.where(last, 1, 0))

    row_meta = [remote(table.at[blk], table.at[blk], meta_send.at[k - 1], meta_recv.at[k - 1], beside(k)) for k in range(1, SIDE)]
    for copy in row_meta:
        copy.start()
    gathers = [[remote(patches.at[pl.ds(1, HELD), strip(across(k)), lanes(i)], pool[i].at[pl.ds(HELD * place, HELD)],
                       pool_send.at[i, k - 1], pool_recv.at[i, k - 1], beside(k)) for k in range(1, SIDE)] for i in range(PARTS)]
    for part in gathers:
        for copy in part:
            copy.start()

    for copy in ends:
        copy.wait()
    edges[0] = corner[0, pl.ds(0, 1), :]
    edges[1] = corner[1, pl.ds(7, 1), :]

    for copy in row_meta:
        copy.wait_recv()
    own_row = pl.ds(row * SIDE, SIDE)
    column_meta = [remote(table.at[own_row], table.at[own_row], meta_send.at[SIDE - 2 + k], meta_recv.at[SIDE - 2 + k], over(k)) for k in range(1, rows_of_devices)]
    for copy in column_meta:
        copy.start()
    upper = remote(edges.at[0], planes.at[1], plane_send, plane_recv.at[1], before)
    upper.start()
    base = remote(edges.at[1], bases.at[place], base_send, base_recv.at[place], (grp, row * SIDE + SIDE - 1))
    base_here = pltpu.make_async_copy(edges.at[1], bases.at[SIDE - 1], base_send)
    @pl.when(jnp.logical_not(last))
    def _():
        base.start()
    @pl.when(last)
    def _():
        base_here.start()
    for copy in column_meta:
        copy.wait_recv()
    read = pltpu.make_async_copy(table, numbers, small.at[2])
    read.start()
    read.wait()

    def number(rank, column):
        return numbers[lax.rem(row * SIDE + rank - 1 + devices, devices), 0, column]

    live = [number(rank, 0) for rank in range(SIDE + 1)]
    for s in range(STEPS):
        sent = [number(rank, 1 + s) for rank in range(SIDE + 1)]
        cut = [have - gone for have, gone in zip(live, sent)]
        for rank in range(SIDE + 1):
            cuts[8 * s + rank] = cut[rank] if rank else FAR
            above[8 * s + rank] = cut[rank - 1] if rank > 1 else OWN + MOST * s
        live = [cut[0]] + [cut[rank] + sent[rank - 1] for rank in range(1, SIDE + 1)]

    def traced(rank, slot, steps):
        for s in reversed(range(steps)):
            beyond = slot - cuts[8 * s + rank]
            came = beyond >= 0
            slot = jnp.where(came, above[8 * s + rank] + beyond, slot)
            rank = jnp.where(came, rank - 1, rank)
            rank = jnp.maximum(rank, 0)
        return jnp.where(rank == 0, slot, HELD * (rank - 1) + slot - 1)

    for s in range(STEPS):
        for t in range(MOST):
            slot = cuts[8 * s + SIDE] + t
            wanted[32 + MOST * s + t] = jnp.clip(traced(jnp.int32(SIDE), slot, s), 0, OWN - 1)

    crosses = [remote(crossing_out[i], crossing_in[i], cross_send.at[i], cross_recv.at[i], over(1)) for i in range(PARTS)]

    def cross(i):
        local[i].wait()
        for copy in gathers[i]:
            copy.wait_recv()
        for n in range(CROSS):
            crossing_out[i][n] = pool[i][wanted[32 + n]]
        crosses[i].start()

    cross(0)

    def plan(n, carry):
        rank, slot = lax.div(n, HELD) + 1, lax.rem(n, HELD) + 1
        wanted[n] = jnp.clip(traced(rank, slot, STEPS), 0, OWN + CROSS - 1)
        return carry
    lax.fori_loop(0, OWN, plan, 0)

    def moved_by(rank):
        total = numbers[rank, 0, 1]
        for s in range(1, STEPS):
            total = total + numbers[rank, 0, 1 + s]
        return total

    gone_before = moved_by(lax.rem(blk + devices - 1, devices))
    info[0] = numbers[blk, 0, 0] - moved_by(blk) + gone_before
    lower_counts = jnp.int32(0)
    for rank in range(devices):
        lower_counts = lower_counts + jnp.where(rank < blk, numbers[rank, 0, 0], 0)
    info[1] = jnp.where(blk == 0, 0, lower_counts - gone_before + moved_by(devices - 1))
    info[2] = jnp.where(line > 0, 1, 0)
    info[3] = jnp.where(line < groups * devices - 1, 1, 0)

    for i in range(1, PARTS):
        cross(i)

    scatters = [[remote(final[i].at[pl.ds(HELD * across(k), HELD)], moved.at[:, strip(place), lanes(i)],
                        final_send.at[i, k - 1], final_recv.at[i, k - 1], beside(k)) for k in range(1, SIDE)] for i in range(PARTS)]
    stays = [pltpu.make_async_copy(final[i].at[pl.ds(HELD * place, HELD)], moved.at[:, strip(place), lanes(i)], final_local.at[i]) for i in range(PARTS)]
    @pl.when(last)
    def _():
        for k in range(SIDE - 1):
            remote(edges.at[1], bases.at[k], base_send, base_recv.at[k], beside(1)).wait_recv()
        base_here.wait()
    for i in range(PARTS):
        crosses[i].wait_recv()
        def pick(n, carry, i=i):
            source = wanted[n]
            own = pool[i][jnp.minimum(source, OWN - 1)]
            other = crossing_in[i][jnp.maximum(source - OWN, 0)]
            final[i][n] = jnp.where(source < OWN, own, other)
            return carry
        lax.fori_loop(0, OWN, pick, 0, unroll=7)
        for copy in scatters[i]:
            copy.start()
        stays[i].start()
        @pl.when(last)
        def _():
            for k in range(SIDE):
                top = final[i][HELD * k + jnp.maximum(live[k + 1] - 2, 0), pl.ds(depth - 1, 1), :]
                tops[k, :, lanes(i)] = jnp.where(live[k + 1] > 1, top, bases[k, :, lanes(i)])
    top_copies = [remote(tops.at[k], planes.at[0], top_send.at[k], plane_recv.at[0], beside(k + 2)) for k in range(SIDE - 2)]
    top_copies.append(remote(tops.at[SIDE - 1], planes.at[0], top_send.at[SIDE - 1], plane_recv.at[0], after))
    top_here = pltpu.make_async_copy(tops.at[SIDE - 2], planes.at[0], plane_recv.at[0])
    @pl.when(last)
    def _():
        for copy in top_copies:
            copy.start()
        top_here.start()
        for copy in top_copies:
            copy.wait_send()
    @pl.when(jnp.logical_not(last))
    def _():
        base.wait_send()
    top_copies[0].wait_recv()
    upper.wait()
    for copy in row_meta + column_meta:
        copy.wait_send()
    for i in range(PARTS):
        crosses[i].wait_send()
        for copy in gathers[i]:
            copy.wait_send()
        stays[i].wait()
        for copy in scatters[i]:
            copy.wait()

def exchange(counts, moves, patches):
    slots, edge, width = patches.shape
    part = width // PARTS
    strip = edge // SIDE
    def blocks(number):
        return [pltpu.VMEM((number, strip, part), jnp.float32)] * PARTS
    dma = pltpu.SemaphoreType.DMA
    others = SIDE - 1
    return pl.pallas_call(
        exchange_kernel,
        out_shape=(jax.ShapeDtypeStruct((HELD, edge, width), jnp.float32),
                   jax.ShapeDtypeStruct((2, 1, width), jnp.float32),
                   jax.ShapeDtypeStruct((8,), jnp.int32)),
        in_specs=[pl.BlockSpec(memory_space=pltpu.SMEM)] * 2 + [pl.BlockSpec(memory_space=pl.ANY)],
        out_specs=(pl.BlockSpec(memory_space=pl.ANY), pl.BlockSpec(memory_space=pl.ANY), pl.BlockSpec(memory_space=pltpu.SMEM)),
        scratch_shapes=blocks(OWN) + blocks(CROSS) + blocks(CROSS) + blocks(OWN) + [
            pltpu.VMEM((16, 1, 128), jnp.int32), pltpu.SMEM((16, 1, 128), jnp.int32),
            pltpu.SMEM((8 * STEPS,), jnp.int32), pltpu.SMEM((8 * STEPS,), jnp.int32), pltpu.SMEM((48,), jnp.int32),
            pltpu.VMEM((2, 8, width), jnp.float32), pltpu.VMEM((2, 1, width), jnp.float32),
            pltpu.VMEM((SIDE, 1, width), jnp.float32), pltpu.VMEM((SIDE, 1, width), jnp.float32),
            dma((PARTS, others)), dma((PARTS, others)), dma((PARTS,)), dma((PARTS,)), dma((PARTS,)),
            dma((PARTS, others)), dma((PARTS, others)), dma((PARTS,)),
            dma((2 * others,)), dma((2 * others,)), dma((3,)), dma(()), dma((2,)), dma(()), dma((SIDE,)), dma((SIDE,)),
        ],
        compiler_params=pltpu.CompilerParams(collective_id=0, has_side_effects=True),
        name="exchange",
    )(counts, moves, patches)


def refine_weights():
    fine = np.arange(64)
    home, side = fine // 2, fine // 2 + 2 * (fine % 2) - 1
    grid = np.arange(32)[:, None]
    z = 0.75 * (grid == home) + 0.25 * (grid == side)
    y = np.zeros((4, 2, 2), np.float32)
    for c in range(2):
        y[c + 1, c, :] = 0.75
        y[c, c, 0] = 0.25
        y[c + 2, c, 1] = 0.25
    half = np.kron(y.reshape(4, 4), z)
    return np.concatenate([half, half], 0)

def refine_kernel(info, tags, patches, moved, planes, weights, fine, rows, stage, done, in_sem, out_sem):
    slots, edge = patches.shape[0], patches.shape[1]
    loads = [pltpu.make_async_copy(moved.at[j - 1] if j else patches.at[0], rows.at[pl.ds(8 + edge * j, edge)], in_sem.at[j]) for j in range(slots)]
    for load in loads:
        load.start()
    live, offset = info[0], info[1]
    for load in loads:
        load.wait()
    rows[pl.ds(7, 1), :] = jnp.where(info[2] == 0, 0.0, planes[0])
    rows[pl.ds(8 + edge * live, 1), :] = jnp.where(info[3] == 0, 0.0, planes[1])
    lanes = lax.broadcasted_iota(jnp.int32, (2 * edge, 128), 1)
    zeros = jnp.zeros((2 * edge, 128), jnp.float32)

    def one(j, carry):
        start = pl.multiple_of(edge * j, 8)
        tag = tags[0, jnp.minimum(offset + j, tags.shape[1] - 1)]
        factor = jnp.where(j < live, 1.0 + 0.5 * tag.astype(jnp.float32), 0.0)
        for m in range(8):
            part = rows[pl.ds(start, edge + 16), pl.ds(128 * m, 128)] * factor
            home = 0.75 * part[8:8 + edge]
            quarter = 0.25 * part
            stage[m, pl.ds(0, edge, stride=2), :] = home + quarter[7:7 + edge]
            stage[m, pl.ds(1, edge, stride=2), :] = home + quarter[9:9 + edge]
        def emit(window, value):
            high = value.astype(jnp.bfloat16)
            low = (value - high.astype(jnp.float32)).astype(jnp.bfloat16)
            both = jnp.concatenate([high, low], axis=1)
            got = jnp.dot(both, weights[...], preferred_element_type=jnp.float32)
            done[j, :, pl.ds(256 * window, 256)] = got.astype(jnp.bfloat16)
        right_before = zeros
        tile = stage[0]
        left = pltpu.roll(tile, 96, 1)
        for m in range(8):
            right = pltpu.roll(tile, 32, 1)
            emit(2 * m, jnp.where(lanes < 32, right_before, right))
            right_before = right
            if m < 7:
                tile = stage[m + 1]
                left_next = pltpu.roll(tile, 96, 1)
            else:
                left_next = zeros
            emit(2 * m + 1, jnp.where(lanes < 96, left, left_next))
            left = left_next
        pltpu.make_async_copy(done.at[j], fine.at[j], out_sem.at[j]).start()
        return carry

    lax.fori_loop(0, slots, one, 0)
    for j in range(slots):
        pltpu.make_async_copy(done.at[j], fine.at[j], out_sem.at[j]).wait()

def refine(info, tags, patches, moved, planes, weights):
    return pl.pallas_call(
        refine_kernel,
        out_shape=jax.ShapeDtypeStruct((8, 64, 4096), jnp.bfloat16),
        in_specs=[pl.BlockSpec(memory_space=pltpu.SMEM)] * 2 + [pl.BlockSpec(memory_space=pl.ANY)] * 2 + [pl.BlockSpec(memory_space=pltpu.VMEM)] * 2,
        out_specs=pl.BlockSpec(memory_space=pl.ANY),
        scratch_shapes=[pltpu.VMEM((272, 1024), jnp.float32), pltpu.VMEM((8, 64, 128), jnp.float32),
                        pltpu.VMEM((8, 64, 4096), jnp.bfloat16),
                        pltpu.SemaphoreType.DMA((8,)), pltpu.SemaphoreType.DMA((8,))],
        name="refine",
    )(info, tags, patches, moved, planes, weights)


def body(patches, counts, moves, tags):
    moved, planes, info = exchange(counts, moves, patches)
    weights = jnp.asarray(refine_weights(), jnp.bfloat16)
    return refine(info, tags, patches, moved, planes, weights)


def solution(mesh):
    in_specs = (
        P(("grp", "blk"), None, None),
        P(("grp", "blk")),
        P(("grp", "blk"), None),
        P("grp", None),
    )
    out_specs = P(("grp", "blk"), None, None)
    return jax.shard_map(body, mesh=mesh, in_specs=in_specs, out_specs=out_specs, check_vma=False)
```

time: 89 us -> 41.1 us (0.46)
  the two profiles are of different devices: /device:TPU:127 before, /device:TPU:1 now
where the time goes in v2:
time: 41.1 us; the launch traced here: 40.5 us
  Pallas kernels  39.9 us (97%)
  between operations  0.66 us (2%)
    pallas_call x1, Pallas kernels, exchange(): pl.pallas_call(exchange_kernel, out_shape=(jax.ShapeDtypeStruct((HELD, ed...  32.3 us
    pallas_call x1, Pallas kernels, refine(): pl.pallas_call(refine_kernel, out_shape=jax.ShapeDtypeStruct((8, 64, 4096...  7.58 us

profile of v2, /device:TPU:1, one launch (start us, length us, event | category | flops | bytes accessed | tf_op | source)
XLA Modules:
  0.0 40.5 jit_solution(14840743816485577258)
XLA Ops:
  0.7 32.3 %exchange.1 = (f32[7,32,1024]{2,1,0:T(8,128)}, f32[2,1,1024]{2,1,0:T(1,128)}, s32[8]{0:T(128)}) custom-call(s32[1]{0:T(128)S(6)} %copy.6.counts, s32[1,4]{1,0:T(1,128)} %moves.1, f32[8,32,1024]{2,1,0:T(8,128)} %patches.3), custom_call_target="tpu_custom_call" | custom-call | tf_op jit(solution)/shard_map/exchange/pallas_call | solution.py:241
  33.0 7.6 %refine.1 = bf16[8,64,4096]{2,1,0:T(8,128)(2,1)} custom-call(s32[8]{0:T(128)} %get-tuple-element.8.info, s32[1,128]{1,0:T(1,128)} %tags.1, f32[8,32,1024]{2,1,0:T(8,128)} %patches.3, f32[7,32,1024]{2,1,0:T(8,128)} %get-tuple-element.9.moved, f32[2,1,1024]{2,1,0:T(1,128)} %get-tuple-element.10.planes, bf16[256,256]{1,0:T(8,128)(2,1)} %constant.2.clone.weights), custom_call_target="tpu_custom_call" | custom-call | tf_op jit(solution)/shard_map/refine/pallas_call | solution.py:326

commit v3 on v2

--- a/solution.py
+++ b/solution.py
@@ -96,9 +96,11 @@
     edges[0] = corner[0, pl.ds(0, 1), :]
     edges[1] = corner[1, pl.ds(7, 1), :]
 
+    own_row = pl.ds(row * SIDE, SIDE)
     for copy in row_meta:
         copy.wait_recv()
-    own_row = pl.ds(row * SIDE, SIDE)
+    read_row = pltpu.make_async_copy(table.at[own_row], numbers.at[own_row], small.at[2])
+    read_row.start()
     column_meta = [remote(table.at[own_row], table.at[own_row], meta_send.at[SIDE - 2 + k], meta_recv.at[SIDE - 2 + k], over(k)) for k in range(1, rows_of_devices)]
     for copy in column_meta:
         copy.start()
@@ -112,23 +114,27 @@
     @pl.when(last)
     def _():
         base_here.start()
-    for copy in column_meta:
-        copy.wait_recv()
-    read = pltpu.make_async_copy(table, numbers, small.at[2])
-    read.start()
-    read.wait()
+    read_row.wait()
 
     def number(rank, column):
         return numbers[lax.rem(row * SIDE + rank - 1 + devices, devices), 0, column]
 
-    live = [number(rank, 0) for rank in range(SIDE + 1)]
+    def levels(known):
+        live = [number(rank, 0) for rank in range(1, SIDE + 1)]
+        for s in range(STEPS):
+            sent = [number(rank, 1 + s) for rank in range(1, SIDE + 1)]
+            came = [number(0, 1 + s) if known else 0] + sent[:-1]
+            cut = [have - gone for have, gone in zip(live, sent)]
+            for rank in range(1, SIDE + 1):
+                cuts[8 * s + rank] = cut[rank - 1]
+                above[8 * s + rank] = cut[rank - 2] if rank > 1 else OWN + MOST * s
+            live = [stay + new for stay, new in zip(cut, came)]
+        return live
+
     for s in range(STEPS):
-        sent = [number(rank, 1 + s) for rank in range(SIDE + 1)]
-        cut = [have - gone for have, gone in zip(live, sent)]
-        for rank in range(SIDE + 1):
-            cuts[8 * s + rank] = cut[rank] if rank else FAR
-            above[8 * s + rank] = cut[rank - 1] if rank > 1 else OWN + MOST * s
-        live = [cut[0]] + [cut[rank] + sent[rank - 1] for rank in range(1, SIDE + 1)]
+        cuts[8 * s] = FAR
+        above[8 * s] = 0
+    levels(False)
 
     def traced(rank, slot, steps):
         for s in reversed(range(steps)):
@@ -156,28 +162,20 @@
 
     cross(0)
 
+    for copy in column_meta:
+        copy.wait_recv()
+    read = pltpu.make_async_copy(table, numbers, small.at[3])
+    read.start()
+    read.wait()
+    live = levels(True)
+
     def plan(n, carry):
         rank, slot = lax.div(n, HELD) + 1, lax.rem(n, HELD) + 1
         wanted[n] = jnp.clip(traced(rank, slot, STEPS), 0, OWN + CROSS - 1)
         return carry
     lax.fori_loop(0, OWN, plan, 0)
 
-    def moved_by(rank):
-        total = numbers[rank, 0, 1]
-        for s in range(1, STEPS):
-            total = total + numbers[rank, 0, 1 + s]
-        return total
-
-    gone_before = moved_by(lax.rem(blk + devices - 1, devices))
-    info[0] = numbers[blk, 0, 0] - moved_by(blk) + gone_before
-    lower_counts = jnp.int32(0)
-    for rank in range(devices):
-        lower_counts = lower_counts + jnp.where(rank < blk, numbers[rank, 0, 0], 0)
-    info[1] = jnp.where(blk == 0, 0, lower_counts - gone_before + moved_by(devices - 1))
-    info[2] = jnp.where(line > 0, 1, 0)
-    info[3] = jnp.where(line < groups * devices - 1, 1, 0)
-
-    for i in range(1, PARTS):
+    for i in range(1, PARTS - 1):
         cross(i)
 
     scatters = [[remote(final[i].at[pl.ds(HELD * across(k), HELD)], moved.at[:, strip(place), lanes(i)],
@@ -189,6 +187,8 @@
             remote(edges.at[1], bases.at[k], base_send, base_recv.at[k], beside(1)).wait_recv()
         base_here.wait()
     for i in range(PARTS):
+        if i == 1:
+            cross(PARTS - 1)
         crosses[i].wait_recv()
         def pick(n, carry, i=i):
             source = wanted[n]
@@ -203,8 +203,23 @@
         @pl.when(last)
         def _():
             for k in range(SIDE):
-                top = final[i][HELD * k + jnp.maximum(live[k + 1] - 2, 0), pl.ds(depth - 1, 1), :]
-                tops[k, :, lanes(i)] = jnp.where(live[k + 1] > 1, top, bases[k, :, lanes(i)])
+                top = final[i][HELD * k + jnp.maximum(live[k] - 2, 0), pl.ds(depth - 1, 1), :]
+                tops[k, :, lanes(i)] = jnp.where(live[k] > 1, top, bases[k, :, lanes(i)])
+    def moved_by(rank):
+        total = numbers[rank, 0, 1]
+        for s in range(1, STEPS):
+            total = total + numbers[rank, 0, 1 + s]
+        return total
+
+    gone_before = moved_by(lax.rem(blk + devices - 1, devices))
+    info[0] = numbers[blk, 0, 0] - moved_by(blk) + gone_before
+    lower_counts = jnp.int32(0)
+    for rank in range(devices):
+        lower_counts = lower_counts + jnp.where(rank < blk, numbers[rank, 0, 0], 0)
+    info[1] = jnp.where(blk == 0, 0, lower_counts - gone_before + moved_by(devices - 1))
+    info[2] = jnp.where(line > 0, 1, 0)
+    info[3] = jnp.where(line < groups * devices - 1, 1, 0)
+
     top_copies = [remote(tops.at[k], planes.at[0], top_send.at[k], plane_recv.at[0], beside(k + 2)) for k in range(SIDE - 2)]
     top_copies.append(remote(tops.at[SIDE - 1], planes.at[0], top_send.at[SIDE - 1], plane_recv.at[0], after))
     top_here = pltpu.make_async_copy(tops.at[SIDE - 2], planes.at[0], plane_recv.at[0])
@@ -252,7 +267,7 @@
             pltpu.VMEM((SIDE, 1, width), jnp.float32), pltpu.VMEM((SIDE, 1, width), jnp.float32),
             dma((PARTS, others)), dma((PARTS, others)), dma((PARTS,)), dma((PARTS,)), dma((PARTS,)),
             dma((PARTS, others)), dma((PARTS, others)), dma((PARTS,)),
-            dma((2 * others,)), dma((2 * others,)), dma((3,)), dma(()), dma((2,)), dma(()), dma((SIDE,)), dma((SIDE,)),
+            dma((2 * others,)), dma((2 * others,)), dma((4,)), dma(()), dma((2,)), dma(()), dma((SIDE,)), dma((SIDE,)),
         ],
         compiler_params=pltpu.CompilerParams(collective_id=0, has_side_effects=True),
         name="exchange",
@@ -318,7 +333,7 @@
         pltpu.make_async_copy(done.at[j], fine.at[j], out_sem.at[j]).start()
         return carry
 
-    lax.fori_loop(0, slots, one, 0)
+    lax.fori_loop(0, slots, one, 0, unroll=4)
     for j in range(slots):
         pltpu.make_async_copy(done.at[j], fine.at[j], out_sem.at[j]).wait()
 

time: 41.1 us -> 39.5 us (0.961); the launches traced: 40.5 us -> 39.4 us
  Pallas kernels: 39.9 us -> 38.7 us
    pallas_call x1, Pallas kernels: 7.58 us -> 6.48 us  [refine(): pl.pallas_call(refine_kernel, out_shape=jax.ShapeDtypeStruct((8, 64, 4096...]
where the time goes in v3:
time: 39.5 us; the launch traced here: 39.4 us
  Pallas kernels  38.7 us (98%)
  between operations  0.66 us (2%)
    pallas_call x1, Pallas kernels, exchange(): pl.pallas_call(exchange_kernel, out_shape=(jax.ShapeDtypeStruct((HELD, ed...  32.2 us
    pallas_call x1, Pallas kernels, refine(): pl.pallas_call(refine_kernel, out_shape=jax.ShapeDtypeStruct((8, 64, 4096...  6.48 us

profile of v3, /device:TPU:1, one launch (start us, length us, event | category | flops | bytes accessed | tf_op | source)
XLA Modules:
  0.0 39.4 jit_solution(2478679701196214288)
XLA Ops:
  0.7 32.2 %exchange.1 = (f32[7,32,1024]{2,1,0:T(8,128)}, f32[2,1,1024]{2,1,0:T(1,128)}, s32[8]{0:T(128)}) custom-call(s32[1]{0:T(128)S(6)} %copy.6.counts, s32[1,4]{1,0:T(1,128)} %moves.1, f32[8,32,1024]{2,1,0:T(8,128)} %patches.3), custom_call_target="tpu_custom_call" | custom-call | tf_op jit(solution)/shard_map/exchange/pallas_call | solution.py:256
  32.9 6.5 %refine.1 = bf16[8,64,4096]{2,1,0:T(8,128)(2,1)} custom-call(s32[8]{0:T(128)} %get-tuple-element.8.info, s32[1,128]{1,0:T(1,128)} %tags.1, f32[8,32,1024]{2,1,0:T(8,128)} %patches.3, f32[7,32,1024]{2,1,0:T(8,128)} %get-tuple-element.9.moved, f32[2,1,1024]{2,1,0:T(1,128)} %get-tuple-element.10.planes, bf16[256,256]{1,0:T(8,128)(2,1)} %constant.2.clone.weights), custom_call_target="tpu_custom_call" | custom-call | tf_op jit(solution)/shard_map/refine/pallas_call | solution.py:341

commit v4 on v3

--- a/solution.py
+++ b/solution.py
@@ -17,16 +17,17 @@
 PARTS = 4
 FAR = 1000
 
-def exchange_kernel(counts, moves, patches, moved, planes, info, *scratch):
+def exchange_kernel(counts_in, moves_in, patches, moved, planes, info_out, *scratch):
     scratch = list(scratch)
     def take(number):
         out = scratch[:number]
         del scratch[:number]
         return out
+    counts, moves, info = take(3)
     pool, crossing_in, crossing_out, final = take(PARTS), take(PARTS), take(PARTS), take(PARTS)
     table, numbers, cuts, above, wanted, corner, edges, bases, tops = take(9)
     (pool_send, pool_recv, pool_local, cross_send, cross_recv, final_send, final_recv, final_local,
-     meta_send, meta_recv, small, plane_send, plane_recv, base_send, base_recv, top_send) = scratch
+     meta_send, meta_recv, small, plane_send, plane_recv, base_send, base_recv, top_send, ready) = scratch
 
     grp, blk = lax.axis_index("grp"), lax.axis_index("blk")
     groups, devices = lax.axis_size("grp"), lax.axis_size("blk")
@@ -57,30 +58,45 @@
     def strip(home):
         return pl.ds(pl.multiple_of(home * depth, depth), depth)
 
+    first, last = place == 0, place == SIDE - 1
+    opening, closing = blk == 0, blk == devices - 1
+    next_group = (lax.rem(grp + 1, groups), 0)
+    last_group = (lax.rem(grp + groups - 1, groups), 0)
+    barrier = pltpu.get_barrier_semaphore()
+    for k in range(1, SIDE):
+        pl.semaphore_signal(barrier, inc=1, device_id=beside(k), device_id_type=MESH)
+    for k in range(1, rows_of_devices):
+        pl.semaphore_signal(barrier, inc=1, device_id=over(k), device_id_type=MESH)
+    @pl.when(last)
+    def _():
+        pl.semaphore_signal(barrier, inc=1, device_id=(grp, lax.rem(blk + 1, devices)), device_id_type=MESH)
+    @pl.when(first)
+    def _():
+        pl.semaphore_signal(barrier, inc=1, device_id=(grp, lax.rem(blk + devices - 1, devices)), device_id_type=MESH)
+    @pl.when(opening)
+    def _():
+        pl.semaphore_signal(barrier, inc=1, device_id=next_group, device_id_type=MESH)
+        pl.semaphore_signal(barrier, inc=1, device_id=last_group, device_id_type=MESH)
+
     local = [pltpu.make_async_copy(patches.at[pl.ds(1, HELD), strip(place), lanes(i)], pool[i].at[pl.ds(HELD * place, HELD)], pool_local.at[i]) for i in range(PARTS)]
     ends = [pltpu.make_async_copy(patches.at[0, pl.ds(0, 8)], corner.at[0], small.at[0]),
             pltpu.make_async_copy(patches.at[0, pl.ds(patches.shape[1] - 8, 8)], corner.at[1], small.at[1])]
-    for copy in ends + local:
+    given = [pltpu.make_async_copy(counts_in, counts, small.at[4]), pltpu.make_async_copy(moves_in, moves, small.at[5])]
+    for copy in given + ends + local:
         copy.start()
+    for copy in given:
+        copy.wait()
     lane = lax.broadcasted_iota(jnp.int32, (1, 128), 1)
     mine = jnp.where(lane == 0, counts[0], 0)
     for s in range(STEPS):
         mine = jnp.where(lane == 1 + s, moves[0, s], mine)
     table[blk] = mine
 
-    barrier = pltpu.get_barrier_semaphore()
-    for k in range(1, SIDE):
-        pl.semaphore_signal(barrier, inc=1, device_id=beside(k), device_id_type=MESH)
-    for k in range(1, rows_of_devices):
-        pl.semaphore_signal(barrier, inc=1, device_id=over(k), device_id_type=MESH)
-    first, last = place == 0, place == SIDE - 1
-    @pl.when(last)
-    def _():
-        pl.semaphore_signal(barrier, inc=1, device_id=after, device_id_type=MESH)
-    @pl.when(first)
-    def _():
-        pl.semaphore_signal(barrier, inc=1, device_id=before, device_id_type=MESH)
-    pl.semaphore_wait(barrier, SIDE - 1 + rows_of_devices - 1 + jnp.where(first, 1, 0) + jnp.where(last, 1, 0))
+    pl.semaphore_wait(barrier, SIDE - 1 + rows_of_devices - 1 + jnp.where(first, 1, 0) + jnp.where(last, 1, 0) + jnp.where(opening, 2, 0))
+    @pl.when(opening)
+    def _():
+        pl.semaphore_signal(ready, inc=1, device_id=(grp, devices - 1), device_id_type=MESH)
+        pl.semaphore_signal(ready, inc=1, device_id=next_group, device_id_type=MESH)
 
     row_meta = [remote(table.at[blk], table.at[blk], meta_send.at[k - 1], meta_recv.at[k - 1], beside(k)) for k in range(1, SIDE)]
     for copy in row_meta:
@@ -105,7 +121,6 @@
     for copy in column_meta:
         copy.start()
     upper = remote(edges.at[0], planes.at[1], plane_send, plane_recv.at[1], before)
-    upper.start()
     base = remote(edges.at[1], bases.at[place], base_send, base_recv.at[place], (grp, row * SIDE + SIDE - 1))
     base_here = pltpu.make_async_copy(edges.at[1], bases.at[SIDE - 1], base_send)
     @pl.when(jnp.logical_not(last))
@@ -162,6 +177,10 @@
 
     cross(0)
 
+    @pl.when(opening)
+    def _():
+        pl.semaphore_wait(ready, 1)
+    upper.start()
     for copy in column_meta:
         copy.wait_recv()
     read = pltpu.make_async_copy(table, numbers, small.at[3])
@@ -219,10 +238,17 @@
     info[1] = jnp.where(blk == 0, 0, lower_counts - gone_before + moved_by(devices - 1))
     info[2] = jnp.where(line > 0, 1, 0)
     info[3] = jnp.where(line < groups * devices - 1, 1, 0)
+    for n in range(4, 8):
+        info[n] = 0
+    tell = pltpu.make_async_copy(info, info_out, small.at[6])
+    tell.start()
 
     top_copies = [remote(tops.at[k], planes.at[0], top_send.at[k], plane_recv.at[0], beside(k + 2)) for k in range(SIDE - 2)]
     top_copies.append(remote(tops.at[SIDE - 1], planes.at[0], top_send.at[SIDE - 1], plane_recv.at[0], after))
     top_here = pltpu.make_async_copy(tops.at[SIDE - 2], planes.at[0], plane_recv.at[0])
+    @pl.when(closing)
+    def _():
+        pl.semaphore_wait(ready, 1)
     @pl.when(last)
     def _():
         for copy in top_copies:
@@ -235,6 +261,7 @@
         base.wait_send()
     top_copies[0].wait_recv()
     upper.wait()
+    tell.wait()
     for copy in row_meta + column_meta:
         copy.wait_send()
     for i in range(PARTS):
@@ -258,16 +285,16 @@
         out_shape=(jax.ShapeDtypeStruct((HELD, edge, width), jnp.float32),
                    jax.ShapeDtypeStruct((2, 1, width), jnp.float32),
                    jax.ShapeDtypeStruct((8,), jnp.int32)),
-        in_specs=[pl.BlockSpec(memory_space=pltpu.SMEM)] * 2 + [pl.BlockSpec(memory_space=pl.ANY)],
-        out_specs=(pl.BlockSpec(memory_space=pl.ANY), pl.BlockSpec(memory_space=pl.ANY), pl.BlockSpec(memory_space=pltpu.SMEM)),
-        scratch_shapes=blocks(OWN) + blocks(CROSS) + blocks(CROSS) + blocks(OWN) + [
+        in_specs=[pl.BlockSpec(memory_space=pl.ANY)] * 3,
+        out_specs=(pl.BlockSpec(memory_space=pl.ANY),) * 3,
+        scratch_shapes=[pltpu.SMEM((1,), jnp.int32), pltpu.SMEM((1, STEPS), jnp.int32), pltpu.SMEM((8,), jnp.int32)] + blocks(OWN) + blocks(CROSS) + blocks(CROSS) + blocks(OWN) + [
             pltpu.VMEM((16, 1, 128), jnp.int32), pltpu.SMEM((16, 1, 128), jnp.int32),
             pltpu.SMEM((8 * STEPS,), jnp.int32), pltpu.SMEM((8 * STEPS,), jnp.int32), pltpu.SMEM((48,), jnp.int32),
             pltpu.VMEM((2, 8, width), jnp.float32), pltpu.VMEM((2, 1, width), jnp.float32),
             pltpu.VMEM((SIDE, 1, width), jnp.float32), pltpu.VMEM((SIDE, 1, width), jnp.float32),
             dma((PARTS, others)), dma((PARTS, others)), dma((PARTS,)), dma((PARTS,)), dma((PARTS,)),
             dma((PARTS, others)), dma((PARTS, others)), dma((PARTS,)),
-            dma((2 * others,)), dma((2 * others,)), dma((4,)), dma(()), dma((2,)), dma(()), dma((SIDE,)), dma((SIDE,)),
+            dma((2 * others,)), dma((2 * others,)), dma((7,)), dma(()), dma((2,)), dma(()), dma((SIDE,)), dma((SIDE,)), pltpu.SemaphoreType.REGULAR,
         ],
         compiler_params=pltpu.CompilerParams(collective_id=0, has_side_effects=True),
         name="exchange",
@@ -287,35 +314,48 @@
     half = np.kron(y.reshape(4, 4), z)
     return np.concatenate([half, half], 0)
 
-def refine_kernel(info, tags, patches, moved, planes, weights, fine, rows, stage, done, in_sem, out_sem):
+def refine_kernel(info_in, tags_in, patches, moved, planes_in, weights_in, fine, info, tags, planes, weights, rows, stage, done, in_sem, small_sem, out_sem):
     slots, edge = patches.shape[0], patches.shape[1]
     loads = [pltpu.make_async_copy(moved.at[j - 1] if j else patches.at[0], rows.at[pl.ds(8 + edge * j, edge)], in_sem.at[j]) for j in range(slots)]
-    for load in loads:
+    small = [pltpu.make_async_copy(src, dst, small_sem.at[n]) for n, (src, dst) in enumerate([(info_in, info), (tags_in, tags), (planes_in, planes), (weights_in, weights)])]
+    for load in small + loads:
         load.start()
+    for load in small[:3]:
+        load.wait()
     live, offset = info[0], info[1]
-    for load in loads:
-        load.wait()
     rows[pl.ds(7, 1), :] = jnp.where(info[2] == 0, 0.0, planes[0])
-    rows[pl.ds(8 + edge * live, 1), :] = jnp.where(info[3] == 0, 0.0, planes[1])
-    lanes = lax.broadcasted_iota(jnp.int32, (2 * edge, 128), 1)
-    zeros = jnp.zeros((2 * edge, 128), jnp.float32)
-
-    def one(j, carry):
-        start = pl.multiple_of(edge * j, 8)
-        tag = tags[0, jnp.minimum(offset + j, tags.shape[1] - 1)]
-        factor = jnp.where(j < live, 1.0 + 0.5 * tag.astype(jnp.float32), 0.0)
-        for m in range(8):
-            part = rows[pl.ds(start, edge + 16), pl.ds(128 * m, 128)] * factor
-            home = 0.75 * part[8:8 + edge]
-            quarter = 0.25 * part
-            stage[m, pl.ds(0, edge, stride=2), :] = home + quarter[7:7 + edge]
-            stage[m, pl.ds(1, edge, stride=2), :] = home + quarter[9:9 + edge]
+    rows[pl.ds(8 + edge * slots, 1), :] = jnp.zeros((1, rows.shape[1]), jnp.float32)
+    small[3].wait()
+    group = 2
+    lanes = lax.broadcasted_iota(jnp.int32, (2 * edge * group, 128), 1)
+    zeros = jnp.zeros((2 * edge * group, 128), jnp.float32)
+
+    first_row = lax.broadcasted_iota(jnp.int32, (8, 128), 0) == 0
+
+    def some(g):
+        for load in loads[0 if g == 0 else group * g + 1:group * g + group + 1]:
+            load.wait()
+        for half in range(group):
+            j = g * group + half
+            start = edge * j
+            tag = tags[0, jnp.minimum(offset + j, tags.shape[1] - 1)]
+            factor = jnp.where(j < live, 1.0 + 0.5 * tag.astype(jnp.float32), 0.0)
+            top = j == live - 1
+            for m in range(8):
+                chunk = pl.ds(128 * m, 128)
+                over = jnp.where(info[3] == 0, 0.0, planes[1, :, chunk])
+                tail = jnp.where(jnp.logical_and(top, first_row), over, rows[pl.ds(start + edge + 8, 8), chunk])
+                part = jnp.concatenate([rows[pl.ds(start, edge + 8), chunk], tail], 0) * factor
+                home = 0.75 * part[8:8 + edge]
+                quarter = 0.25 * part
+                stage[m, pl.ds(2 * edge * half, edge, stride=2), :] = home + quarter[7:7 + edge]
+                stage[m, pl.ds(2 * edge * half + 1, edge, stride=2), :] = home + quarter[9:9 + edge]
         def emit(window, value):
             high = value.astype(jnp.bfloat16)
             low = (value - high.astype(jnp.float32)).astype(jnp.bfloat16)
             both = jnp.concatenate([high, low], axis=1)
             got = jnp.dot(both, weights[...], preferred_element_type=jnp.float32)
-            done[j, :, pl.ds(256 * window, 256)] = got.astype(jnp.bfloat16)
+            done[pl.ds(g * group, group), :, pl.ds(256 * window, 256)] = got.astype(jnp.bfloat16).reshape(group, 2 * edge, 256)
         right_before = zeros
         tile = stage[0]
         left = pltpu.roll(tile, 96, 1)
@@ -330,10 +370,12 @@
                 left_next = zeros
             emit(2 * m + 1, jnp.where(lanes < 96, left, left_next))
             left = left_next
-        pltpu.make_async_copy(done.at[j], fine.at[j], out_sem.at[j]).start()
-        return carry
-
-    lax.fori_loop(0, slots, one, 0, unroll=4)
+        for half in range(group):
+            j = g * group + half
+            pltpu.make_async_copy(done.at[j], fine.at[j], out_sem.at[j]).start()
+
+    for g in range(slots // group):
+        some(g)
     for j in range(slots):
         pltpu.make_async_copy(done.at[j], fine.at[j], out_sem.at[j]).wait()
 
@@ -341,11 +383,13 @@
     return pl.pallas_call(
         refine_kernel,
         out_shape=jax.ShapeDtypeStruct((8, 64, 4096), jnp.bfloat16),
-        in_specs=[pl.BlockSpec(memory_space=pltpu.SMEM)] * 2 + [pl.BlockSpec(memory_space=pl.ANY)] * 2 + [pl.BlockSpec(memory_space=pltpu.VMEM)] * 2,
+        in_specs=[pl.BlockSpec(memory_space=pl.ANY)] * 6,
         out_specs=pl.BlockSpec(memory_space=pl.ANY),
-        scratch_shapes=[pltpu.VMEM((272, 1024), jnp.float32), pltpu.VMEM((8, 64, 128), jnp.float32),
+        scratch_shapes=[pltpu.SMEM((8,), jnp.int32), pltpu.SMEM((1, 128), jnp.int32),
+                        pltpu.VMEM((2, 1, 1024), jnp.float32), pltpu.VMEM((256, 256), jnp.bfloat16),
+                        pltpu.VMEM((272, 1024), jnp.float32), pltpu.VMEM((8, 128, 128), jnp.float32),
                         pltpu.VMEM((8, 64, 4096), jnp.bfloat16),
-                        pltpu.SemaphoreType.DMA((8,)), pltpu.SemaphoreType.DMA((8,))],
+                        pltpu.SemaphoreType.DMA((8,)), pltpu.SemaphoreType.DMA((4,)), pltpu.SemaphoreType.DMA((8,))],
         name="refine",
     )(info, tags, patches, moved, planes, weights)
 

time: 39.5 us -> 36 us (0.911)
  Pallas kernels: 38.7 us -> 35.2 us
    pallas_call x1, Pallas kernels: 6.48 us -> 4.52 us  [refine(): pl.pallas_call(refine_kernel, out_shape=jax.ShapeDtypeStruct((8, 64, 4096...]
    pallas_call x1, Pallas kernels: 32.2 us -> 30.6 us  [exchange(): pl.pallas_call(exchange_kernel, out_shape=(jax.ShapeDtypeStruct((HELD, ed...]
where the time goes in v4:
time: 36 us; the launch traced here: 35.8 us
  Pallas kernels  35.2 us (98%)
  between operations  0.66 us (2%)
    pallas_call x1, Pallas kernels, exchange(): pl.pallas_call(exchange_kernel, out_shape=(jax.ShapeDtypeStruct((HELD, ed...  30.6 us
    pallas_call x1, Pallas kernels, refine(): pl.pallas_call(refine_kernel, out_shape=jax.ShapeDtypeStruct((8, 64, 4096...  4.52 us

profile of v4, /device:TPU:1, one launch (start us, length us, event | category | flops | bytes accessed | tf_op | source)
XLA Modules:
  0.0 35.8 jit_solution(2035588562114877823)
XLA Ops:
  0.7 30.6 %exchange.1 = (f32[7,32,1024]{2,1,0:T(8,128)}, f32[2,1,1024]{2,1,0:T(1,128)}, s32[8]{0:T(128)}) custom-call(s32[1]{0:T(128)S(6)} %copy.6.counts_in, s32[1,4]{1,0:T(1,128)} %moves_in.1, f32[8,32,1024]{2,1,0:T(8,128)} %patches.3), custom_call_target="tpu_custom_call" | custom-call | tf_op jit(solution)/shard_map/exchange/pallas_call | solution.py:283
  31.3 4.5 %refine.1 = bf16[8,64,4096]{2,1,0:T(8,128)(2,1)} custom-call(s32[8]{0:T(128)} %get-tuple-element.8.info_in, s32[1,128]{1,0:T(1,128)} %tags_in.1, f32[8,32,1024]{2,1,0:T(8,128)} %patches.3, f32[7,32,1024]{2,1,0:T(8,128)} %get-tuple-element.9.moved, f32[2,1,1024]{2,1,0:T(1,128)} %get-tuple-element.10.planes_in, bf16[256,256]{1,0:T(8,128)(2,1)} %constant.2.clone.weights_in), custom_call_target="tpu_custom_call" | custom-call | tf_op jit(solution)/shard_map/refine/pallas_call | solution.py:383

commit v5 on v4

--- a/solution.py
+++ b/solution.py
@@ -331,6 +331,10 @@
     zeros = jnp.zeros((2 * edge * group, 128), jnp.float32)
 
     first_row = lax.broadcasted_iota(jnp.int32, (8, 128), 0) == 0
+
+    def leave(g, piece):
+        part = (pl.ds(g * group, group), slice(None), pl.ds(1024 * piece, 1024))
+        return pltpu.make_async_copy(done.at[part], fine.at[part], out_sem.at[g, piece])
 
     def some(g):
         for load in loads[0 if g == 0 else group * g + 1:group * g + group + 1]:
@@ -370,14 +374,13 @@
                 left_next = zeros
             emit(2 * m + 1, jnp.where(lanes < 96, left, left_next))
             left = left_next
-        for half in range(group):
-            j = g * group + half
-            pltpu.make_async_copy(done.at[j], fine.at[j], out_sem.at[j]).start()
-
+            if m % 2:
+                leave(g, m // 2).start()
     for g in range(slots // group):
         some(g)
-    for j in range(slots):
-        pltpu.make_async_copy(done.at[j], fine.at[j], out_sem.at[j]).wait()
+    for g in range(slots // group):
+        for piece in range(4):
+            leave(g, piece).wait()
 
 def refine(info, tags, patches, moved, planes, weights):
     return pl.pallas_call(
@@ -389,7 +392,7 @@
                         pltpu.VMEM((2, 1, 1024), jnp.float32), pltpu.VMEM((256, 256), jnp.bfloat16),
                         pltpu.VMEM((272, 1024), jnp.float32), pltpu.VMEM((8, 128, 128), jnp.float32),
                         pltpu.VMEM((8, 64, 4096), jnp.bfloat16),
-                        pltpu.SemaphoreType.DMA((8,)), pltpu.SemaphoreType.DMA((4,)), pltpu.SemaphoreType.DMA((8,))],
+                        pltpu.SemaphoreType.DMA((8,)), pltpu.SemaphoreType.DMA((4,)), pltpu.SemaphoreType.DMA((4, 4))],
         name="refine",
     )(info, tags, patches, moved, planes, weights)
 

time: 36 us -> 35.8 us (level)
  no operation moved by 1% of the time
where the time goes in v5:
time: 35.8 us; the launch traced here: 35.7 us
  Pallas kernels  35 us (98%)
  between operations  0.66 us (2%)
    pallas_call x1, Pallas kernels, exchange(): pl.pallas_call(exchange_kernel, out_shape=(jax.ShapeDtypeStruct((HELD, ed...  30.6 us
    pallas_call x1, Pallas kernels, refine(): pl.pallas_call(refine_kernel, out_shape=jax.ShapeDtypeStruct((8, 64, 4096...  4.38 us

profile of v5, /device:TPU:1, one launch (start us, length us, event | category | flops | bytes accessed | tf_op | source)
XLA Modules:
  0.0 35.7 jit_solution(4184762385324419993)
XLA Ops:
  0.7 30.6 %exchange.1 = (f32[7,32,1024]{2,1,0:T(8,128)}, f32[2,1,1024]{2,1,0:T(1,128)}, s32[8]{0:T(128)}) custom-call(s32[1]{0:T(128)S(6)} %copy.6.counts_in, s32[1,4]{1,0:T(1,128)} %moves_in.1, f32[8,32,1024]{2,1,0:T(8,128)} %patches.3), custom_call_target="tpu_custom_call" | custom-call | tf_op jit(solution)/shard_map/exchange/pallas_call | solution.py:283
  31.3 4.4 %refine.1 = bf16[8,64,4096]{2,1,0:T(8,128)(2,1)} custom-call(s32[8]{0:T(128)} %get-tuple-element.8.info_in, s32[1,128]{1,0:T(1,128)} %tags_in.1, f32[8,32,1024]{2,1,0:T(8,128)} %patches.3, f32[7,32,1024]{2,1,0:T(8,128)} %get-tuple-element.9.moved, f32[2,1,1024]{2,1,0:T(1,128)} %get-tuple-element.10.planes_in, bf16[256,256]{1,0:T(8,128)(2,1)} %constant.2.clone.weights_in), custom_call_target="tpu_custom_call" | custom-call | tf_op jit(solution)/shard_map/refine/pallas_call | solution.py:386

commit v6 on v5

--- a/solution.py
+++ b/solution.py
@@ -15,6 +15,7 @@
 OWN = SIDE * HELD
 CROSS = MOST * STEPS
 PARTS = 4
+FAR_FIRST = (1, 0, 2)
 FAR = 1000
 
 def exchange_kernel(counts_in, moves_in, patches, moved, planes, info_out, *scratch):
@@ -104,8 +105,8 @@
     gathers = [[remote(patches.at[pl.ds(1, HELD), strip(across(k)), lanes(i)], pool[i].at[pl.ds(HELD * place, HELD)],
                        pool_send.at[i, k - 1], pool_recv.at[i, k - 1], beside(k)) for k in range(1, SIDE)] for i in range(PARTS)]
     for part in gathers:
-        for copy in part:
-            copy.start()
+        for n in FAR_FIRST:
+            part[n].start()
 
     for copy in ends:
         copy.wait()
@@ -216,8 +217,8 @@
             final[i][n] = jnp.where(source < OWN, own, other)
             return carry
         lax.fori_loop(0, OWN, pick, 0, unroll=7)
-        for copy in scatters[i]:
-            copy.start()
+        for n in FAR_FIRST:
+            scatters[i][n].start()
         stays[i].start()
         @pl.when(last)
         def _():
@@ -352,8 +353,8 @@
                 part = jnp.concatenate([rows[pl.ds(start, edge + 8), chunk], tail], 0) * factor
                 home = 0.75 * part[8:8 + edge]
                 quarter = 0.25 * part
-                stage[m, pl.ds(2 * edge * half, edge, stride=2), :] = home + quarter[7:7 + edge]
-                stage[m, pl.ds(2 * edge * half + 1, edge, stride=2), :] = home + quarter[9:9 + edge]
+                stage[g % 2, m, pl.ds(2 * edge * half, edge, stride=2), :] = home + quarter[7:7 + edge]
+                stage[g % 2, m, pl.ds(2 * edge * half + 1, edge, stride=2), :] = home + quarter[9:9 + edge]
         def emit(window, value):
             high = value.astype(jnp.bfloat16)
             low = (value - high.astype(jnp.float32)).astype(jnp.bfloat16)
@@ -361,14 +362,14 @@
             got = jnp.dot(both, weights[...], preferred_element_type=jnp.float32)
             done[pl.ds(g * group, group), :, pl.ds(256 * window, 256)] = got.astype(jnp.bfloat16).reshape(group, 2 * edge, 256)
         right_before = zeros
-        tile = stage[0]
+        tile = stage[g % 2, 0]
         left = pltpu.roll(tile, 96, 1)
         for m in range(8):
             right = pltpu.roll(tile, 32, 1)
             emit(2 * m, jnp.where(lanes < 32, right_before, right))
             right_before = right
             if m < 7:
-                tile = stage[m + 1]
+                tile = stage[g % 2, m + 1]
                 left_next = pltpu.roll(tile, 96, 1)
             else:
                 left_next = zeros
@@ -390,7 +391,7 @@
         out_specs=pl.BlockSpec(memory_space=pl.ANY),
         scratch_shapes=[pltpu.SMEM((8,), jnp.int32), pltpu.SMEM((1, 128), jnp.int32),
                         pltpu.VMEM((2, 1, 1024), jnp.float32), pltpu.VMEM((256, 256), jnp.bfloat16),
-                        pltpu.VMEM((272, 1024), jnp.float32), pltpu.VMEM((8, 128, 128), jnp.float32),
+                        pltpu.VMEM((272, 1024), jnp.float32), pltpu.VMEM((2, 8, 128, 128), jnp.float32),
                         pltpu.VMEM((8, 64, 4096), jnp.bfloat16),
                         pltpu.SemaphoreType.DMA((8,)), pltpu.SemaphoreType.DMA((4,)), pltpu.SemaphoreType.DMA((4, 4))],
         name="refine",

time: 35.8 us -> 35.8 us (level)
  the two profiles are of different devices: /device:TPU:1 before, /device:TPU:200 now
where the time goes in v6:
time: 35.8 us; the launch traced here: 35.6 us
  Pallas kernels  35 us (98%)
  between operations  0.66 us (2%)
    pallas_call x1, Pallas kernels, exchange(): pl.pallas_call(exchange_kernel, out_shape=(jax.ShapeDtypeStruct((HELD, ed...  30.6 us
    pallas_call x1, Pallas kernels, refine(): pl.pallas_call(refine_kernel, out_shape=jax.ShapeDtypeStruct((8, 64, 4096...  4.38 us

profile of v6, /device:TPU:200, one launch (start us, length us, event | category | flops | bytes accessed | tf_op | source)
XLA Modules:
  0.0 35.6 jit_solution(360744352451115528)
XLA Ops:
  0.7 30.6 %exchange.1 = (f32[7,32,1024]{2,1,0:T(8,128)}, f32[2,1,1024]{2,1,0:T(1,128)}, s32[8]{0:T(128)}) custom-call(s32[1]{0:T(128)S(6)} %copy.6.counts_in, s32[1,4]{1,0:T(1,128)} %moves_in.1, f32[8,32,1024]{2,1,0:T(8,128)} %patches.3), custom_call_target="tpu_custom_call" | custom-call | tf_op jit(solution)/shard_map/exchange/pallas_call | solution.py:284
  31.2 4.4 %refine.1 = bf16[8,64,4096]{2,1,0:T(8,128)(2,1)} custom-call(s32[8]{0:T(128)} %get-tuple-element.8.info_in, s32[1,128]{1,0:T(1,128)} %tags_in.1, f32[8,32,1024]{2,1,0:T(8,128)} %patches.3, f32[7,32,1024]{2,1,0:T(8,128)} %get-tuple-element.9.moved, f32[2,1,1024]{2,1,0:T(1,128)} %get-tuple-element.10.planes_in, bf16[256,256]{1,0:T(8,128)(2,1)} %constant.2.clone.weights_in), custom_call_target="tpu_custom_call" | custom-call | tf_op jit(solution)/shard_map/refine/pallas_call | solution.py:387
